TPU v7x, 512 devices: a whole 4x8x8 slice. The times are simulated.
512 devices in a mesh: head: 16 (over x, z_lo), ctx: 32 (over y, z_hi, core).
Axes of the slice: x: 4, y: 8, z: 8 (z_hi: 2, z_lo: 4; z = z_hi * 4 + z_lo), core: 2. Of those that a mesh axis runs over, the one named last changes fastest.
Arguments:
- queries: bfloat16 [64, 128, 2048], P('ctx', 'head'), may hold values from -8 to 8
- key_vectors: bfloat16 [64, 128, 256], P('ctx', 'head'), may hold values from -8 to 8
- value_vectors: bfloat16 [64, 128, 256], P('ctx', 'head'), may hold values from -4 to 4
- out_grad: bfloat16 [64, 128, 2048], P('ctx', 'head'), may hold values from -4 to 4
- block_order: int32 [64], replicated, may hold values from 0 to 63, each once
Outputs:
- attended: bfloat16 [64, 128, 2048], P('ctx', 'head')
- query_grad: bfloat16 [64, 128, 2048], P('ctx', 'head')
- key_grad: bfloat16 [64, 128, 256], P('ctx', 'head')
- value_grad: bfloat16 [64, 128, 256], P('ctx', 'head')
All inputs are finite; a program needn't handle non-finite values.
Results may differ from a plain program's by a relative error of at most 0.025.
Values may be sent and summed in bfloat16 or wider, within the bound.
A program may use at most 64 MiB of HBM per device.

v0:
```python
import math

import jax
import jax.numpy as jnp
from jax import lax
from jax.sharding import PartitionSpec as P

HD = 128


LOWEST = -1e30


def row_positions(block_order, first_row, row_count, block_len):
    row_index = first_row + jnp.arange(row_count, dtype=jnp.int32)
    block_id = row_index // block_len
    matches = block_id[:, None] == jnp.arange(block_order.shape[0], dtype=jnp.int32)[None, :]
    picked = jnp.sum(jnp.where(matches, block_order[None, :], 0), axis=1)
    return picked * block_len + row_index % block_len


def contract_rows(left_side, right_side):
    return lax.dot_general(
        left_side, right_side, (((1,), (1,)), ((), ())), preferred_element_type=jnp.float32
    )


def contract_cols(left_side, right_side):
    return lax.dot_general(
        left_side, right_side, (((0,), (0,)), ((), ())), preferred_element_type=jnp.float32
    )


def forward_tile(running, key_part, value_part, part_pos, query_rows, query_pos, scaling):
    row_max, row_sum, weighted = running
    scores = contract_rows(query_rows, key_part) * scaling
    allowed = part_pos[None, :] <= query_pos[:, None]
    new_max = jnp.maximum(row_max, jnp.max(jnp.where(allowed, scores, LOWEST), axis=1))
    weights = jnp.where(allowed, jnp.exp(scores - new_max[:, None]), 0.0)
    factor = jnp.exp(row_max - new_max)
    weighted = weighted * factor[:, None] + jnp.dot(
        weights.astype(jnp.bfloat16), value_part, preferred_element_type=jnp.float32
    )
    return (new_max, row_sum * factor + jnp.sum(weights, axis=1), weighted)


def backward_tile(
    key_part, value_part, query_part, grad_part, log_part, delta_part, part_pos, own_data, scaling
):
    query_rows, grad_rows, query_pos, key_rows, value_rows, key_pos, log_total, row_delta = own_data
    head_size = key_rows.shape[1]
    per_row = query_part.shape[1] // head_size
    remote_pos = jnp.repeat(part_pos, per_row)
    remote_log = log_part.reshape(-1)
    remote_delta = delta_part.reshape(-1)
    scores = contract_rows(query_rows, key_part) * scaling
    allowed = part_pos[None, :] <= query_pos[:, None]
    probs = jnp.where(allowed, jnp.exp(scores - log_total[:, None]), 0.0)
    grad_weights = contract_rows(grad_rows, value_part)
    grad_scores = (probs * (grad_weights - row_delta[:, None])).astype(jnp.bfloat16)
    query_total = jnp.dot(grad_scores, key_part, preferred_element_type=jnp.float32)
    scores = contract_rows(query_part, key_rows) * scaling
    allowed = key_pos[None, :] <= remote_pos[:, None]
    probs = jnp.where(allowed, jnp.exp(scores - remote_log[:, None]), 0.0)
    grad_weights = contract_rows(grad_part, value_rows)
    grad_scores = (probs * (grad_weights - remote_delta[:, None])).astype(jnp.bfloat16)
    key_total = contract_cols(grad_scores, query_part)
    value_total = contract_cols(probs.astype(jnp.bfloat16), grad_part)
    key_total, value_total = (key_total, value_total)
    return (query_total, key_total, value_total)


def shards(queries, key_vectors, value_vectors, out_grad, block_order):
    head_devices = lax.axis_size("head")
    halves, token_rows, query_width = queries.shape
    kv_heads = key_vectors.shape[2] // HD
    repeat_count = head_devices // kv_heads
    scaling = 1.0 / math.sqrt(HD)

    def widen(source):
        grouped = source.reshape(halves, token_rows, kv_heads, 1, HD)
        return jnp.broadcast_to(grouped, (halves, token_rows, kv_heads, repeat_count, HD)).reshape(
            halves, token_rows, head_devices * HD
        )

    query_local, grad_local, key_local, value_local = (
        lax.all_to_all(queries, "head", split_axis=2, concat_axis=1, tiled=True),
        lax.all_to_all(out_grad, "head", split_axis=2, concat_axis=1, tiled=True),
        lax.all_to_all(widen(key_vectors), "head", split_axis=2, concat_axis=1, tiled=True),
        lax.all_to_all(widen(value_vectors), "head", split_axis=2, concat_axis=1, tiled=True),
    )
    block_len = query_local.shape[1]
    rows_here = halves * block_len
    per_row = query_local.shape[2] // HD
    total_rows = rows_here * per_row
    query_rows = query_local.reshape(total_rows, HD)
    grad_rows = grad_local.reshape(total_rows, HD)
    key_rows = key_local.reshape(rows_here, HD)
    value_rows = value_local.reshape(rows_here, HD)
    key_pos = row_positions(block_order, lax.axis_index("ctx") * rows_here, rows_here, block_len)
    query_pos = jnp.repeat(key_pos, per_row)
    start_state = (
        jnp.full((total_rows,), LOWEST, jnp.float32),
        jnp.zeros((total_rows,), jnp.float32),
        jnp.zeros((total_rows, HD), jnp.float32),
    )

    def forward_piece(running, pieces, first_row):
        key_part, value_part = pieces
        part_pos = row_positions(block_order, first_row, key_part.shape[0], block_len)
        return forward_tile(running, key_part, value_part, part_pos, query_rows, query_pos, scaling)

    whole_keys, whole_values = (
        lax.all_gather(key_rows, "ctx", axis=0, tiled=True),
        lax.all_gather(value_rows, "ctx", axis=0, tiled=True),
    )
    piece_rows = whole_keys.shape[0] // 4

    def forward_step(block_step, running):
        first_row = block_step * piece_rows
        key_part = lax.dynamic_slice_in_dim(whole_keys, first_row, piece_rows, 0)
        value_part = lax.dynamic_slice_in_dim(whole_values, first_row, piece_rows, 0)
        return forward_piece(running, (key_part, value_part), first_row)

    row_max, row_sum, weighted = lax.fori_loop(0, 4, forward_step, start_state)
    log_total = row_max + jnp.log(row_sum)
    attended = (weighted / row_sum[:, None]).astype(jnp.bfloat16)
    attended_wide = lax.optimization_barrier(attended).astype(jnp.float32)
    row_delta = jnp.sum(grad_rows.astype(jnp.float32) * attended_wide, axis=1)
    own_data = (
        query_rows,
        grad_rows,
        query_pos,
        key_rows,
        value_rows,
        key_pos,
        log_total,
        row_delta,
    )
    query_cols = query_local.reshape(rows_here, per_row * HD)
    grad_cols = grad_local.reshape(rows_here, per_row * HD)
    log_cols = log_total.reshape(rows_here, per_row)
    delta_cols = row_delta.reshape(rows_here, per_row)
    all_log, all_delta = (
        lax.all_gather(log_cols, "ctx", axis=0, tiled=True),
        lax.all_gather(delta_cols, "ctx", axis=0, tiled=True),
    )
    query_part = lax.all_gather(query_cols, "ctx", axis=0, tiled=True)
    grad_part = lax.all_gather(grad_cols, "ctx", axis=0, tiled=True)
    row_count = query_part.shape[0]
    part_pos = row_positions(block_order, jnp.int32(0), row_count, block_len)
    key_part = whole_keys
    value_part = whole_values
    query_total, key_total, value_total = backward_tile(
        key_part, value_part, query_part, grad_part, all_log, all_delta, part_pos, own_data, scaling
    )
    query_heads = (query_total * scaling).reshape(halves, block_len, per_row * HD)
    key_heads = (key_total * scaling).reshape(halves, block_len, HD)
    value_heads = value_total.reshape(halves, block_len, HD)
    attended_back, query_back, key_back, value_back = (
        lax.all_to_all(
            attended_wide.reshape(halves, block_len, per_row * HD).astype(jnp.bfloat16),
            "head",
            split_axis=1,
            concat_axis=2,
            tiled=True,
        ).astype(jnp.float32),
        lax.all_to_all(
            query_heads.astype(jnp.bfloat16), "head", split_axis=1, concat_axis=2, tiled=True
        ).astype(query_heads.dtype),
        lax.all_to_all(
            key_heads.astype(jnp.bfloat16), "head", split_axis=1, concat_axis=2, tiled=True
        ).astype(key_heads.dtype),
        lax.all_to_all(
            value_heads.astype(jnp.bfloat16), "head", split_axis=1, concat_axis=2, tiled=True
        ).astype(value_heads.dtype),
    )
    key_sum = jnp.sum(
        key_back.reshape(halves, token_rows, kv_heads, repeat_count, HD), axis=3
    ).reshape(halves, token_rows, kv_heads * HD)
    value_sum = jnp.sum(
        value_back.reshape(halves, token_rows, kv_heads, repeat_count, HD), axis=3
    ).reshape(halves, token_rows, kv_heads * HD)
    return (
        attended_back.astype(jnp.bfloat16),
        query_back.astype(jnp.bfloat16),
        key_sum.astype(jnp.bfloat16),
        value_sum.astype(jnp.bfloat16),
    )


def solution(mesh):
    placed = (
        P("ctx", "head", None),
        P("ctx", "head", None),
        P("ctx", "head", None),
        P("ctx", "head", None),
        P(),
    )
    return jax.shard_map(
        shards,
        mesh=mesh,
        in_specs=placed,
        out_specs=(
            P("ctx", "head", None),
            P("ctx", "head", None),
            P("ctx", "head", None),
            P("ctx", "head", None),
        ),
        check_vma=False,
    )
```

profile of v0, /device:TPU:1, one launch (start us, length us, event | category | flops | bytes accessed | tf_op | source)
XLA Modules:
  0.0 441.0 jit_solution(2521501416507460304)
XLA Ops:
  10.0 17.2 %all_to_all.114 = bf16[16,2,1024]{2,1,0:T(2,128)(2,1)S(1)} all-to-all(bf16[16,2,1024]{2,1,0:T(2,128)(2,1)S(1)} %reshape.214), channel_id=1, replica_groups=mesh['head'=16,'ctx'=32] {'head'}, dimensions={0} | all-to-all | bytes 131072 | tf_op jit(solution)/shard_map/all_to_all | solution.py:89
  32.2 9.6 %all_to_all.115 = bf16[16,2,1024]{2,1,0:T(2,128)(2,1)S(1)} all-to-all(bf16[16,2,1024]{2,1,0:T(2,128)(2,1)S(1)} %reshape.218), channel_id=1, replica_groups=mesh['head'=16,'ctx'=32] {'head'}, dimensions={0} | all-to-all | bytes 131072 | tf_op jit(solution)/shard_map/all_to_all | solution.py:90
  46.6 9.5 %all_to_all.116 = bf16[16,2,1024]{2,1,0:T(2,128)(2,1)S(1)} all-to-all(bf16[16,2,1024]{2,1,0:T(2,128)(2,1)S(1)} %reshape.216), channel_id=1, replica_groups=mesh['head'=16,'ctx'=32] {'head'}, dimensions={0} | all-to-all | bytes 131072 | tf_op jit(solution)/shard_map/all_to_all | solution.py:87
  61.6 3.5 all-to-all-start.4
  65.9 6.1 %all-to-all-done.4 = bf16[16,2,1024]{2,1,0:T(2,128)(2,1)S(1)} async-done(((bf16[16,2,1024]{2,1,0:T(2,128)(2,1)}), bf16[16,2,1024]{2,1,0:T(2,128)(2,1)S(1)}, u32[]{:S(2)}, u32[]{:S(2)}) %all-to-all-start.4) | async-done | bytes 65568 | tf_op jit(solution)/shard_map/all_to_all | solution.py:88
  74.9 51.5 %all-gather.9.cloned.1.call-done = bf16[8192,128]{1,0:T(8,128)(2,1)} async-done(((bf16[256,128]{1,0:T(8,128)(2,1)}), bf16[8192,128]{1,0:T(8,128)(2,1)}) %all-gather.9.cloned.1.call-update) | async-done | bytes 2097168 | tf_op jit(solution)/shard_map/all_gather | solution.py:114
  126.4 91.0 %all-gather.11.cloned.1.call-done = bf16[8192,128]{1,0:T(8,128)(2,1)} async-done(((bf16[256,128]{1,0:T(8,128)(2,1)}), bf16[8192,128]{1,0:T(8,128)(2,1)}) %all-gather.11.cloned.1.call-update) | async-done | bytes 2097168 | tf_op jit(solution)/shard_map/all_gather | solution.py:115
  217.3 17.3 %while.20 = (s32[]{:T(128)}, f32[256]{0:T(256)S(1)}, f32[256]{0:T(256)S(1)}, f32[256,128]{1,0:T(8,128)S(1)}, s32[64]{0:T(128)S(1)}, /*index=5*/s32[256]{0:T(256)...) while((s32[]{:T(128)}, f32[256]{0:T(256)S(1)}, ...), condition=%wide.region_5.6_spmd.clone, body=%wide.region_1.5_spmd.clone.sunk | while | flops 275279104 | bytes 7753167 | solution.py:125
  224.1 1.9 convolution_add_fusion.2
  228.5 1.9 convolution_add_fusion.2
  235.5 4.5 %all-to-all-start.3 = ((bf16[2,128,128]{2,0,1:T(2,128)(2,1)}), bf16[2,128,128]{2,0,1:T(2,128)(2,1)S(1)}, u32[]{:S(2)}, u32[]{:S(2)}) async-start(bf16[2,128,128]{2,0,1:T(2,128)(2,1)} %copy.74), calls=%async_computation.3 | async-start | bytes 131072 | tf_op jit(solution)/shard_map/all_to_all | solution.py:161
  240.0 49.9 %all-gather.2 = f32[32,1,256]{2,1,0:T(1,128)S(1)} all-gather(f32[1,1,256]{2,1,0:T(1,128)S(1)} %bitcast.114), channel_id=2, replica_groups=mesh['head'=16,'ctx'=32] {'ctx'}, dimensions={0}, use_global_device_ids=true | all-gather | bytes 33792 | tf_op jit(solution)/shard_map/all_gather | solution.py:145
  290.1 7.2 %fusion.27 = f32[256,8192]{1,0:T(8,128)} fusion(bf16[256,128]{1,0:T(8,128)(2,1)S(1)} %get-tuple-element.404, bf16[8192,128]{1,0:T(8,128)(2,1)} %get-tuple-element.392, f32[256]{0:T(256)S(1)} %log_add_fusion, s32[8192]{0:T(1024)S(1)} %fusion.48, s32[256]{0:T(256)S(1)} %get-tuple-element.410), kind=kOutput, calls=%fused_computation.47 | convolution fusion | flops 545259520 | bytes 10586112 | tf_op jit(solution)/shard_map/dot_general | solution.py:23
  297.2 6.5 %fusion.37 = bf16[256,128]{1,0:T(8,128)(2,1)S(1)} fusion(bf16[8192,128]{1,0:T(8,128)(2,1)S(1)} %copy-done.1, f32[256,8192]{1,0:T(8,128)} %fusion.27, bf16[256,128]{1,0:T(8,128)(2,1)S(1)} %bitcast.90, bf16[8192,128]{1,0:T(8,128)(2,1)} %get-tuple-element.395, f32[256]{0:T(256)S(1)} %multiply_reduce_fusion), kind=kOutput, calls=%fused_computation.59 | convolution fusion | flops 1080098816 | bytes 12715008 | tf_op jit(solution)/shard_map/dot_general | solution.py:61
  303.7 5.3 %all-gather.13.cloned.1.call-done = bf16[8192,128]{1,0:T(8,128)(2,1)} async-done(((bf16[256,128]{1,0:T(8,128)(2,1)}), bf16[8192,128]{1,0:T(8,128)(2,1)}) %all-gather.13.cloned.1.call-update) | async-done | bytes 2097168 | tf_op jit(solution)/shard_map/all_gather | solution.py:148
  309.0 7.6 %fusion.28 = f32[8192,256]{1,0:T(8,128)} fusion(bf16[8192,128]{1,0:T(8,128)(2,1)} %all-gather.13.cloned.1.call-done, bf16[256,128]{1,0:T(8,128)(2,1)S(1)} %bitcast.99, f32[8192]{0:T(1024)S(1)} %bitcast.108, s32[256]{0:T(256)S(1)} %get-tuple-element.410, s32[8192]{0:T(1024)S(1)} %fusion.48), kind=kOutput, calls=%fused_computation.48 | convolution fusion | flops 545259520 | bytes 10617856 | tf_op jit(solution)/shard_map/dot_general | solution.py:23
  317.3 47.5 %all-gather.3 = f32[32,1,256]{2,1,0:T(1,128)S(1)} all-gather(f32[1,1,256]{2,1,0:T(1,128)S(1)} %bitcast.109), channel_id=3, replica_groups=mesh['head'=16,'ctx'=32] {'ctx'}, dimensions={0}, use_global_device_ids=true | all-gather | bytes 33792 | tf_op jit(solution)/shard_map/all_gather | solution.py:146
  364.9 6.3 %all-to-all-start.5 = ((bf16[2,128,128]{2,0,1:T(2,128)(2,1)}), bf16[2,128,128]{2,0,1:T(2,128)(2,1)S(1)}, u32[]{:S(2)}, u32[]{:S(2)}) async-start(bf16[2,128,128]{2,0,1:T(2,128)(2,1)} %copy.78), calls=%async_computation.5 | async-start | bytes 131072 | tf_op jit(solution)/shard_map/all_to_all | solution.py:168
  371.1 29.5 %all-gather.15.cloned.1.call-done = bf16[8192,128]{1,0:T(8,128)(2,1)} async-done(((bf16[256,128]{1,0:T(8,128)(2,1)}), bf16[8192,128]{1,0:T(8,128)(2,1)}) %all-gather.15.cloned.1.call-update) | async-done | bytes 2097168 | tf_op jit(solution)/shard_map/all_gather | solution.py:149
  400.7 8.6 %fusion.41 = bf16[256,128]{1,0:T(8,128)(2,1)S(1)} fusion(bf16[8192,128]{1,0:T(8,128)(2,1)} %all-gather.13.cloned.1.call-done, f32[8192,256]{1,0:T(8,128)} %fusion.28, bf16[8192,128]{1,0:T(8,128)(2,1)} %all-gather.15.cloned.1.call-done, bf16[256,128]{1,0:T(8,128)(2,1)S(1)} %bitcast.92, f32[8192]{0:T(1024)S(1)} %bitcast.94), kind=kOutput, calls=%fused_computation.61 | convolution fusion | flops 1080098816 | bytes 12746752 | tf_op jit(solution)/shard_map/dot_general | solution.py:29
  410.0 4.4 %all-to-all-start.6 = ((bf16[2,128,128]{2,0,1:T(2,128)(2,1)}), bf16[2,128,128]{2,0,1:T(2,128)(2,1)S(1)}, u32[]{:S(2)}, u32[]{:S(2)}) async-start(bf16[2,128,128]{2,0,1:T(2,128)(2,1)} %copy.80), calls=%async_computation.6 | async-start | bytes 131072 | tf_op jit(solution)/shard_map/all_to_all | solution.py:171
  414.5 4.7 %fusion.38 = bf16[256,128]{1,0:T(8,128)(2,1)S(1)} fusion(bf16[8192,128]{1,0:T(8,128)(2,1)S(1)} %copy-done, f32[8192,256]{1,0:T(8,128)} %fusion.28), kind=kOutput, calls=%fused_computation.60 | convolution fusion | flops 539000832 | bytes 10551296 | tf_op jit(solution)/shard_map/dot_general | solution.py:29
  421.5 5.3 %all-to-all-start.7 = ((bf16[2,128,128]{2,0,1:T(2,128)(2,1)}), bf16[2,128,128]{2,0,1:T(2,128)(2,1)S(1)}, u32[]{:S(2)}, u32[]{:S(2)}) async-start(bf16[2,128,128]{2,0,1:T(2,128)(2,1)} %copy.82), calls=%async_computation.7 | async-start | bytes 131072 | tf_op jit(solution)/shard_map/all_to_all | solution.py:174
  428.8 5.0 %all-to-all-done.7 = bf16[2,128,128]{2,0,1:T(2,128)(2,1)S(1)} async-done(((bf16[2,128,128]{2,0,1:T(2,128)(2,1)}), bf16[2,128,128]{2,0,1:T(2,128)(2,1)S(1)}, u32[]{:S(2)}, u32[]{:S(2)}) %all-to-all-start.7) | async-done | bytes 65568 | tf_op jit(solution)/shard_map/all_to_all | solution.py:174
  (105 shorter events, 42.2 us)
Async XLA Ops:
  7.2 119.2 %all-gather.9.cloned.1.call-start = ((), (), s32[]{:S(2)}) async-start(), calls=%async_computation.8 | async-start | bytes 2162688 | tf_op jit(solution)/shard_map/all_gather | solution.py:114
  8.1 22.0 %copy-start.9 = (bf16[2,8,256]{2,1,0:T(8,128)(2,1)S(1)}, bf16[2,8,256]{2,1,0:T(8,128)(2,1)}, u32[]{:S(2)}) copy-start(bf16[2,8,256]{2,1,0:T(8,128)(2,1)} %param.9) | copy-start | bytes 24580
  30.1 187.3 %all-gather.11.cloned.1.call-start = ((), (), s32[]{:S(2)}) async-start(), calls=%async_computation.9 | async-start | bytes 2162688 | tf_op jit(solution)/shard_map/all_gather | solution.py:115
  30.3 14.5 %copy-start.6 = (bf16[2,8,2048]{2,1,0:T(8,128)(2,1)S(1)}, bf16[2,8,2048]{2,1,0:T(8,128)(2,1)}, u32[]{:S(2)}) copy-start(bf16[2,8,2048]{2,1,0:T(8,128)(2,1)} %param.7) | copy-start | bytes 196612
  44.7 14.4 %copy-start.7 = (bf16[2,8,2048]{2,1,0:T(8,128)(2,1)S(1)}, bf16[2,8,2048]{2,1,0:T(8,128)(2,1)}, u32[]{:S(2)}) copy-start(bf16[2,8,2048]{2,1,0:T(8,128)(2,1)} %param.10) | copy-start | bytes 196612
  44.7 264.3 %all-gather.13.cloned.1.call-start = ((), (), s32[]{:S(2)}) async-start(), calls=%async_computation.10 | async-start | bytes 2162688 | tf_op jit(solution)/shard_map/all_gather | solution.py:148
  56.2 9.2 %copy-start.8 = (s32[64]{0:T(128)S(1)}, s32[64]{0:T(128)}, u32[]{:S(2)}) copy-start(s32[64]{0:T(128)} %param.11) | copy-start | bytes 772
  59.8 157.5 %copy-start.5 = (bf16[2,16,8,128]{3,2,1,0:T(8,128)(2,1)S(1)}, bf16[2,16,8,128]{3,2,1,0:T(8,128)(2,1)}, u32[]{:S(2)}) copy-start(bf16[2,16,8,128]{3,2,1,0:T(8,128)(2,1)} %copy.71) | copy-start | bytes 196612
  61.6 10.4 %all-to-all-start.4 = ((bf16[16,2,1024]{2,1,0:T(2,128)(2,1)}), bf16[16,2,1024]{2,1,0:T(2,128)(2,1)S(1)}, u32[]{:S(2)}, u32[]{:S(2)}) async-start(bf16[16,2,1024]{2,1,0:T(2,128)(2,1)} %reshape.220), calls=%async_computation.4 | async-start | bytes 131072 | tf_op jit(solution)/shard_map/all_to_all | solution.py:88
  65.0 335.6 %all-gather.15.cloned.1.call-start = ((), (), s32[]{:S(2)}) async-start(), calls=%async_computation.11 | async-start | bytes 2162688 | tf_op jit(solution)/shard_map/all_gather | solution.py:149
  217.3 72.6 %copy-start.2 = (bf16[2,8,16,128]{3,1,2,0:T(8,128)(2,1)S(1)}, bf16[2,8,16,128]{3,1,2,0:T(8,128)(2,1)}, u32[]{:S(2)}) copy-start(bf16[2,8,16,128]{3,1,2,0:T(8,128)(2,1)} %copy.77) | copy-start | bytes 196612
  235.5 129.4 %all-to-all-start.3 = ((bf16[2,128,128]{2,0,1:T(2,128)(2,1)}), bf16[2,128,128]{2,0,1:T(2,128)(2,1)S(1)}, u32[]{:S(2)}, u32[]{:S(2)}) async-start(bf16[2,128,128]{2,0,1:T(2,128)(2,1)} %copy.74), calls=%async_computation.3 | async-start | bytes 131072 | tf_op jit(solution)/shard_map/all_to_all | solution.py:161
  290.0 7.2 %copy-start.1 = (bf16[8192,128]{1,0:T(8,128)(2,1)S(1)}, bf16[8192,128]{1,0:T(8,128)(2,1)}, u32[]{:S(2)}) copy-start(bf16[8192,128]{1,0:T(8,128)(2,1)} %get-tuple-element.392) | copy-start | bytes 6291460
  297.2 11.8 %copy-start.4 = (bf16[2,16,8,128]{3,2,1,0:T(8,128)(2,1)S(1)}, bf16[2,16,8,128]{3,2,1,0:T(8,128)(2,1)}, u32[]{:S(2)}) copy-start(bf16[2,16,8,128]{3,2,1,0:T(8,128)(2,1)} %copy.69) | copy-start | bytes 196612
  309.0 91.7 %copy-start.3 = (bf16[2,16,8,128]{3,2,1,0:T(8,128)(2,1)S(1)}, bf16[2,16,8,128]{3,2,1,0:T(8,128)(2,1)}, u32[]{:S(2)}) copy-start(bf16[2,16,8,128]{3,2,1,0:T(8,128)(2,1)} %copy.73) | copy-start | bytes 196612
  364.9 45.2 %all-to-all-start.5 = ((bf16[2,128,128]{2,0,1:T(2,128)(2,1)}), bf16[2,128,128]{2,0,1:T(2,128)(2,1)S(1)}, u32[]{:S(2)}, u32[]{:S(2)}) async-start(bf16[2,128,128]{2,0,1:T(2,128)(2,1)} %copy.78), calls=%async_computation.5 | async-start | bytes 131072 | tf_op jit(solution)/shard_map/all_to_all | solution.py:168
  400.7 13.8 %copy-start = (bf16[8192,128]{1,0:T(8,128)(2,1)S(1)}, bf16[8192,128]{1,0:T(8,128)(2,1)}, u32[]{:S(2)}) copy-start(bf16[8192,128]{1,0:T(8,128)(2,1)} %all-gather.15.cloned.1.call-done) | copy-start | bytes 6291460
  410.0 11.4 %all-to-all-start.6 = ((bf16[2,128,128]{2,0,1:T(2,128)(2,1)}), bf16[2,128,128]{2,0,1:T(2,128)(2,1)S(1)}, u32[]{:S(2)}, u32[]{:S(2)}) async-start(bf16[2,128,128]{2,0,1:T(2,128)(2,1)} %copy.80), calls=%async_computation.6 | async-start | bytes 131072 | tf_op jit(solution)/shard_map/all_to_all | solution.py:171
  421.5 12.3 %all-to-all-start.7 = ((bf16[2,128,128]{2,0,1:T(2,128)(2,1)}), bf16[2,128,128]{2,0,1:T(2,128)(2,1)S(1)}, u32[]{:S(2)}, u32[]{:S(2)}) async-start(bf16[2,128,128]{2,0,1:T(2,128)(2,1)} %copy.82), calls=%async_computation.7 | async-start | bytes 131072 | tf_op jit(solution)/shard_map/all_to_all | solution.py:174
Sparse Core Ops, SparseCore 0:
  30.2 96.1 all-gather.8
  129.7 87.5 all-gather.10
  221.2 87.7 all-gather.12
  312.2 88.4 all-gather.14
where the time goes:
time: 442 us; the launch traced here: 441 us
  waiting for transfers between devices  190 us (43%)
  blocking collectives  134 us (30%)
  matrix products  48.8 us (11%)
  local copies, waits for them, and re-layouts  26 us (6%)
  starting transfers between devices  24.4 us (6%)
  between operations  14.1 us (3%)
    all_gather x1, waiting for transfers between devices, shards(): lax.all_gather(value_rows, 'ctx', axis=0, tiled=True)  91 us
    all_gather x1, waiting for transfers between devices, shards(): lax.all_gather(key_rows, 'ctx', axis=0, tiled=True)  51.5 us
    all_gather x1, blocking collectives, shards(): lax.all_gather(log_cols, 'ctx', axis=0, tiled=True)  49.9 us
    all_gather x1, blocking collectives, shards(): lax.all_gather(delta_cols, 'ctx', axis=0, tiled=True)  47.5 us
    all_gather x1, waiting for transfers between devices, shards(): grad_part = lax.all_gather(grad_cols, 'ctx', axis=0, tiled=True)  29.5 us
    dot_general x6, matrix products, contract_rows(): lax.dot_general(left_side, right_side, (((1,), (1,)), ((), ())), preferre...  21.6 us
    all_to_all x1, blocking collectives, shards(): lax.all_to_all(widen(key_vectors), 'head', split_axis=2, concat_axis=1, t...  17.2 us
    dot_general x2, matrix products, contract_cols(): lax.dot_general(left_side, right_side, (((0,), (0,)), ((), ())), preferre...  13.3 us
  transfers between devices with their start and end apart: 9, of which 7 were waited for; matrix products, arithmetic and copies ran while one was open for 16% of the time, Pallas kernels for 0%

commit v1 on v0

v1 whole, which is shorter than its diff:
```python
import functools
import math

import jax
import jax.numpy as jnp
from jax import lax
from jax.experimental import pallas as pl
from jax.experimental.pallas import tpu as pltpu
from jax.sharding import PartitionSpec as P

HD = 128
GROUP = 8
ROWS = 8
LOWEST = -1e30
MESH = pl.DeviceIdType.MESH
F32 = jnp.float32
BF16 = jnp.bfloat16

SPLIT = dict(x=4, z_lo=4, y=8, z_hi=2)
AHEAD = 3


def matmul(left_side, right_side):
    return lax.dot_general(
        left_side, right_side, (((1,), (0,)), ((), ())), preferred_element_type=F32
    )


def kernel(
    split,
    query_ref, grad_ref, key_ref, value_ref, order_ref,
    attended_out, query_out, key_out, value_out,
    query_all, grad_all, kv_all,
    query_rows, grad_rows, query_cols, grad_cols, key_cols, value_cols,
    key_pos, exps, grad_weights,
    max_rows, sum_rows, dot_rows, ratio_rows, delta_row, stat_all,
    attended_acc, query_acc, out_part, out_in,
    kv_part, sibling_in, y_send, y_in, z_send, z_in,
    q_ss, q_rs, z_ss, z_rs, ring_ss, ring_rs, sib_ss, sib_rs, stat_ss, stat_rs,
    dsib_ss, dsib_rs, dy_ss, dy_rs, dz_ss, dz_rs, out_ss, out_rs, local_sem,
):
    xs, zls, ys, zhs = split["x"], split["z_lo"], split["y"], split["z_hi"]
    zs, srcs = zls * zhs, 2 * xs
    toks = srcs * 2 * ROWS
    cols = GROUP * toks
    keys = 2 * zs * 2 * ROWS
    width = GROUP * HD
    block_len = xs * zls * ROWS
    step = min(256, cols)
    scaling = 1.0 / math.sqrt(HD)
    exp_scale = scaling / math.log(2.0)

    head, ctx = lax.axis_index("head"), lax.axis_index("ctx")
    x, zl = lax.div(head, zls), lax.rem(head, zls)
    core = lax.rem(ctx, 2)
    zh = lax.rem(lax.div(ctx, 2), zhs)
    y = lax.div(ctx, 2 * zhs)
    z = zh * zls + zl
    parity = lax.rem(zl, 2)
    me = x * 2 + parity

    def at(x_to, y_to, z_to, core_to):
        zh_to, zl_to = lax.div(z_to, zls), lax.rem(z_to, zls)
        return {"head": x_to * zls + zl_to, "ctx": (y_to * zhs + zh_to) * 2 + core_to}

    def source(index):
        return at(lax.div(index, 2), y, z - parity + lax.rem(index, 2), core)

    sibling = at(x, y, z, 1 - core)

    def remote(src, dst, send, recv, device):
        return pltpu.make_async_remote_copy(
            src_ref=src, dst_ref=dst, send_sem=send, recv_sem=recv,
            device_id=device, device_id_type=MESH,
        )

    def y_of(order):
        odd = lax.rem(order, 2)
        return lax.rem(
            y + odd * (ys - lax.div(order + 1, 2)) + (1 - odd) * lax.div(order, 2), ys
        )

    barrier = pltpu.get_barrier_semaphore()
    greeted = 1
    pl.semaphore_signal(barrier, inc=1, device_id=sibling, device_id_type=MESH)
    for hop in range(1, srcs):
        other = lax.rem(me + hop, srcs)
        pl.semaphore_signal(barrier, inc=1, device_id=source(other), device_id_type=MESH)
        greeted += 1
    for hop in range(1, ys):
        device = at(x, lax.rem(y + hop, ys), z, core)
        pl.semaphore_signal(barrier, inc=1, device_id=device, device_id_type=MESH)
        greeted += 1
    pair = z - parity
    for hop in range(2, zs):
        device = at(x, y, lax.rem(pair + hop, zs), core)
        pl.semaphore_signal(barrier, inc=1, device_id=device, device_id_type=MESH)
        greeted += 1
    pl.semaphore_wait(barrier, greeted)

    def kv_copy(part, ref, peer, own_slot):
        lanes = pl.ds(pl.multiple_of(lax.rem(peer, 2) * HD, HD), HD)
        return remote(
            ref.at[:, :, lanes], kv_all.at[y, core, part, own_slot],
            z_ss.at[part, peer], z_rs.at[part, own_slot], at(x, y, peer, core),
        )

    def query_copy(part, ref, dst, peer, own_slot):
        lanes = pl.ds(pl.multiple_of(lax.rem(peer, 2) * width, HD), width)
        return remote(
            ref.at[:, :, lanes], dst.at[own_slot],
            q_ss.at[part, peer], q_rs.at[part, own_slot], source(peer),
        )

    kv_refs = (key_ref, value_ref)
    query_refs = ((query_ref, query_all), (grad_ref, grad_all))
    for hop in range(1, zs):
        for part in range(2):
            kv_copy(part, kv_refs[part], lax.rem(z + hop, zs), z).start()
    for hop in range(1, srcs):
        for part in range(2):
            ref, dst = query_refs[part]
            query_copy(part, ref, dst, lax.rem(me + hop, srcs), me).start()
    own = []
    for part in range(2):
        lanes = pl.ds(pl.multiple_of(parity * HD, HD), HD)
        own.append(pltpu.make_async_copy(
            kv_refs[part].at[:, :, lanes], kv_all.at[y, core, part, z], local_sem.at[part]
        ))
        ref, dst = query_refs[part]
        lanes = pl.ds(pl.multiple_of(parity * width, HD), width)
        own.append(pltpu.make_async_copy(ref.at[:, :, lanes], dst.at[me], local_sem.at[2 + part]))
    for copy in own:
        copy.start()

    row_of = lax.broadcasted_iota(jnp.int32, (ROWS, toks), 0)

    def fill_positions(y_at, carry):
        for core_at in range(2):
            for z_at in range(zs):
                for half in range(2):
                    block = ((y_at * zhs + z_at // zls) * 2 + core_at) * 2 + half
                    first = order_ref[block] * block_len + (x * zls + z_at % zls) * ROWS
                    group = (core_at * zs + z_at) * 2 + half
                    key_pos[y_at, group * ROWS:(group + 1) * ROWS, :] = row_of + first
        return carry

    lax.fori_loop(0, ys, fill_positions, 0)
    token = lax.broadcasted_iota(jnp.int32, (1, toks), 1)
    half_of = lax.rem(lax.div(token, ROWS), 2)
    pair_of = lax.rem(lax.div(token, 2 * ROWS), 2)
    x_of = lax.div(token, 4 * ROWS)
    block_pos = jnp.where(half_of == 0, order_ref[ctx * 2], order_ref[ctx * 2 + 1])
    query_pos = (
        block_pos * block_len
        + (x_of * zls + (zl - parity) + pair_of) * ROWS
        + lax.rem(token, ROWS)
    )
    attended_acc[...] = jnp.zeros_like(attended_acc)
    query_acc[...] = jnp.zeros_like(query_acc)

    def ring_copy(order, to_order, to_right, send_slot):
        y_at = y_of(order)
        y_to = lax.rem(y + to_right + (1 - to_right) * (ys - 1), ys)
        return remote(
            kv_all.at[y_at, core], kv_all.at[y_at, core],
            ring_ss.at[send_slot], ring_rs.at[to_order], at(x, y_to, z, core),
        )

    def ring_arrival(order):
        y_at = y_of(order)
        return remote(
            kv_all.at[y_at, core], kv_all.at[y_at, core],
            ring_ss.at[order], ring_rs.at[order], sibling,
        )

    def sibling_copy(order, core_at):
        y_at = y_of(order)
        return remote(
            kv_all.at[y_at, core_at], kv_all.at[y_at, core_at],
            sib_ss.at[order], sib_rs.at[order], sibling,
        )

    def pass_on(order):
        ring_arrival(order).wait_recv()

        @pl.when(order + 2 < ys)
        def _():
            ring_copy(order, order + 2, lax.rem(order, 2), order).start()

        sibling_copy(order, core).start()

    for copy in own:
        copy.wait()
    for hop in range(1, zs):
        peer = lax.rem(z + hop, zs)
        for part in range(2):
            kv_copy(part, kv_refs[part], z, peer).wait_recv()
    ring_copy(0, 1, 1, ys - 1).start()
    if ys > 2:
        ring_copy(0, 2, 0, 0).start()
    sibling_copy(0, core).start()
    for order in range(1, min(AHEAD, ys)):
        pass_on(jnp.int32(order))
    for hop in range(1, srcs):
        peer = lax.rem(me + hop, srcs)
        for part in range(2):
            ref, dst = query_refs[part]
            query_copy(part, ref, dst, me, peer).wait_recv()
    for head_at in range(GROUP):
        lanes = slice(head_at * HD, (head_at + 1) * HD)
        rows = slice(head_at * toks, (head_at + 1) * toks)
        for src, by_row, by_col in (
            (query_all, query_rows, query_cols), (grad_all, grad_rows, grad_cols)
        ):
            tile = src[:, :, :, lanes].astype(F32).reshape(toks, HD)
            by_row[rows, :] = tile.astype(BF16)
            by_col[:, rows] = tile.T.astype(BF16)

    def forward(order, carry):
        @pl.when(order + AHEAD < ys)
        def _():
            pass_on(order + AHEAD)

        sibling_copy(order, 1 - core).wait_recv()
        y_at = y_of(order)
        key_wide = kv_all[y_at, :, 0].astype(F32).reshape(keys, HD)
        value_wide = kv_all[y_at, :, 1].astype(F32).reshape(keys, HD)
        key_cols[y_at] = key_wide.T.astype(BF16)
        value_cols[y_at] = value_wide.T.astype(BF16)
        key_tile, value_tile = key_wide.astype(BF16), value_wide.astype(BF16)
        allowed = jnp.concatenate([key_pos[y_at]] * (step // toks), axis=1) <= jnp.concatenate(
            [query_pos] * (step // toks), axis=1
        )
        for first in range(0, cols, step):
            lanes = slice(first, first + step)
            scores = jnp.where(allowed, matmul(key_tile, query_cols[:, lanes]), LOWEST)
            top = jnp.max(scores, axis=0, keepdims=True)
            exp_tile = jnp.exp2((scores - top) * exp_scale)
            weight_grad = matmul(value_tile, grad_cols[:, lanes])
            exps[y_at, :, lanes] = exp_tile
            grad_weights[y_at, :, lanes] = weight_grad
            max_rows[pl.ds(y_at, 1), lanes] = top
            sum_rows[pl.ds(y_at, 1), lanes] = jnp.sum(exp_tile, axis=0, keepdims=True)
            dot_rows[pl.ds(y_at, 1), lanes] = jnp.sum(
                exp_tile * weight_grad, axis=0, keepdims=True
            )
        return carry

    lax.fori_loop(0, ys, forward, 0)

    top = jnp.max(max_rows[...], axis=0, keepdims=True)
    factor = jnp.exp2((max_rows[...] - top) * exp_scale)
    stat_all[x] = jnp.concatenate(
        [
            top,
            jnp.sum(sum_rows[...] * factor, axis=0, keepdims=True),
            jnp.sum(dot_rows[...] * factor, axis=0, keepdims=True),
            jnp.zeros((5, cols), F32),
        ],
        axis=0,
    )

    def stat_copy(peer, own_slot):
        return remote(
            stat_all.at[own_slot], stat_all.at[own_slot],
            stat_ss.at[peer], stat_rs.at[own_slot], at(peer, y, z, core),
        )

    for hop in range(1, xs):
        stat_copy(lax.rem(x + hop, xs), x).start()
    for hop in range(1, xs):
        stat_copy(x, lax.rem(x + hop, xs)).wait_recv()
    tops = [stat_all[at_x, 0:1, :] for at_x in range(xs)]
    top = functools.reduce(jnp.maximum, tops)
    factors = [jnp.exp2((part - top) * exp_scale) for part in tops]
    total = sum(stat_all[at_x, 1:2, :] * factors[at_x] for at_x in range(xs))
    delta = sum(stat_all[at_x, 2:3, :] * factors[at_x] for at_x in range(xs)) / total
    delta_row[...] = delta
    ratio_rows[...] = jnp.exp2((max_rows[...] - top) * exp_scale) / total

    def dsib_copy(order, core_at):
        return remote(
            kv_part.at[order, core_at], sibling_in.at[order],
            dsib_ss.at[order], dsib_rs.at[order], sibling,
        )

    def dy_copy(order):
        return remote(
            y_send.at[order], y_in.at[order],
            dy_ss.at[order], dy_rs.at[order], at(x, y_of(order), z, core),
        )

    def send_sum(order):
        dsib_copy(order, 1 - core).wait_recv()
        y_send[order] = (
            kv_part[order, core].astype(F32) + sibling_in[order].astype(F32)
        ).astype(BF16)
        dy_copy(order).start()

    def backward(turn, carry):
        order = ys - 1 - turn
        y_at = y_of(order)
        key_sum = jnp.zeros((keys, HD), F32)
        value_sum = jnp.zeros((keys, HD), F32)
        for first in range(0, cols, step):
            lanes = slice(first, first + step)
            probs = exps[y_at, :, lanes] * ratio_rows[pl.ds(y_at, 1), lanes]
            weights = probs.astype(BF16)
            grad_scores = (
                probs * (grad_weights[y_at, :, lanes] - delta_row[:, lanes])
            ).astype(BF16)
            attended_acc[:, lanes] += matmul(value_cols[y_at], weights)
            query_acc[:, lanes] += matmul(key_cols[y_at], grad_scores)
            value_sum += matmul(weights, grad_rows[lanes, :])
            key_sum += matmul(grad_scores, query_rows[lanes, :])
        shape = (2, zs, 2, ROWS, HD)
        kv_part[order, :, 0] = (key_sum * scaling).reshape(shape).astype(BF16)
        kv_part[order, :, 1] = value_sum.reshape(shape).astype(BF16)
        dsib_copy(order, 1 - core).start()

        @pl.when(turn >= 1)
        def _():
            send_sum(order + 1)

        return carry

    lax.fori_loop(0, ys, backward, 0)

    for head_at in range(GROUP):
        lanes = slice(head_at * HD, (head_at + 1) * HD)
        rows = slice(head_at * toks, (head_at + 1) * toks)
        shape = (srcs, 2, ROWS, HD)
        out_part[:, 0, :, :, lanes] = attended_acc[:, rows].T.reshape(shape).astype(BF16)
        out_part[:, 1, :, :, lanes] = (
            (query_acc[:, rows] * scaling).T.reshape(shape).astype(BF16)
        )

    def out_copy(peer, own_slot):
        return remote(
            out_part.at[peer], out_in.at[own_slot],
            out_ss.at[peer], out_rs.at[own_slot], source(peer),
        )

    for hop in range(1, srcs):
        out_copy(lax.rem(me + hop, srcs), me).start()
    out_in[me] = out_part[me]

    dsib_copy(0, 1 - core).wait_recv()
    total_kv = kv_part[0, core].astype(F32) + sibling_in[0].astype(F32)
    for order in range(1, ys):
        dy_copy(order).wait_recv()
        total_kv += y_in[order].astype(F32)
    for part in range(2):
        z_send[:, part] = total_kv[part].astype(BF16)

    def dz_copy(peer, own_slot):
        return remote(
            z_send.at[peer], z_in.at[own_slot],
            dz_ss.at[peer], dz_rs.at[own_slot], at(x, y, peer, core),
        )

    for hop in range(1, zs):
        dz_copy(lax.rem(z + hop, zs), z).start()
    z_in[z] = z_send[z]
    for hop in range(1, srcs):
        out_copy(me, lax.rem(me + hop, srcs)).wait_recv()
    for half in range(2):
        lanes = slice(half * width, (half + 1) * width)
        for part, out in enumerate((attended_out, query_out)):
            out[:, :, lanes] = sum(
                out_in[at_x * 2 + half, part].astype(F32) for at_x in range(xs)
            ).astype(BF16)
    for hop in range(1, zs):
        dz_copy(z, lax.rem(z + hop, zs)).wait_recv()
    for half in range(2):
        lanes = slice(half * HD, (half + 1) * HD)
        for part, out in enumerate((key_out, value_out)):
            out[:, :, lanes] = sum(
                z_in[at_z, part].astype(F32) for at_z in range(half, zs, 2)
            ).astype(BF16)

    for hop in range(1, zs):
        peer = lax.rem(z + hop, zs)
        for part in range(2):
            kv_copy(part, kv_refs[part], peer, z).wait_send()
        dz_copy(peer, z).wait_send()
    for hop in range(1, srcs):
        peer = lax.rem(me + hop, srcs)
        for part in range(2):
            ref, dst = query_refs[part]
            query_copy(part, ref, dst, peer, me).wait_send()
        out_copy(peer, me).wait_send()
    for hop in range(1, xs):
        stat_copy(lax.rem(x + hop, xs), x).wait_send()
    ring_copy(0, 1, 1, ys - 1).wait_send()
    if ys > 2:
        ring_copy(0, 2, 0, 0).wait_send()
    for order in range(1, ys - 2):
        ring_copy(order, order + 2, order % 2, order).wait_send()
    for order in range(ys):
        sibling_copy(order, core).wait_send()
        dsib_copy(order, 1 - core).wait_send()
        if order:
            dy_copy(order).wait_send()


def shards(split, queries, key_vectors, value_vectors, out_grad, block_order):
    xs, zls, ys, zhs = split["x"], split["z_lo"], split["y"], split["z_hi"]
    zs, srcs = zls * zhs, 2 * xs
    toks = srcs * 2 * ROWS
    cols = GROUP * toks
    keys = 2 * zs * 2 * ROWS
    width = GROUP * HD
    vmem = pltpu.VMEM
    dma = pltpu.SemaphoreType.DMA
    kv_block = (2, zs, 2, ROWS, HD)
    whole = pl.BlockSpec(memory_space=pltpu.VMEM)
    return pl.pallas_call(
        functools.partial(kernel, split),
        out_shape=tuple(
            jax.ShapeDtypeStruct(a.shape, BF16)
            for a in (queries, queries, key_vectors, value_vectors)
        ),
        in_specs=[whole] * 4 + [pl.BlockSpec(memory_space=pltpu.SMEM)],
        out_specs=(whole,) * 4,
        scratch_shapes=[
            vmem((srcs, 2, ROWS, width), BF16), vmem((srcs, 2, ROWS, width), BF16),
            vmem((ys, 2) + kv_block, BF16),
            vmem((cols, HD), BF16), vmem((cols, HD), BF16),
            vmem((HD, cols), BF16), vmem((HD, cols), BF16),
            vmem((ys, HD, keys), BF16), vmem((ys, HD, keys), BF16),
            vmem((ys, keys, toks), jnp.int32),
            vmem((ys, keys, cols), F32), vmem((ys, keys, cols), F32),
            vmem((ys, cols), F32), vmem((ys, cols), F32), vmem((ys, cols), F32),
            vmem((ys, cols), F32), vmem((1, cols), F32), vmem((xs, 8, cols), F32),
            vmem((HD, cols), F32), vmem((HD, cols), F32),
            vmem((srcs, 2, 2, ROWS, width), BF16), vmem((srcs, 2, 2, ROWS, width), BF16),
            vmem((ys, 2) + kv_block, BF16), vmem((ys,) + kv_block, BF16),
            vmem((ys,) + kv_block, BF16), vmem((ys,) + kv_block, BF16),
            vmem((zs, 2, 2, ROWS, HD), BF16), vmem((zs, 2, 2, ROWS, HD), BF16),
            dma((2, srcs)), dma((2, srcs)), dma((2, zs)), dma((2, zs)),
            dma((ys,)), dma((ys,)), dma((ys,)), dma((ys,)), dma((xs,)), dma((xs,)),
            dma((ys,)), dma((ys,)), dma((ys,)), dma((ys,)),
            dma((zs,)), dma((zs,)), dma((srcs,)), dma((srcs,)), dma((4,)),
        ],
        compiler_params=pltpu.CompilerParams(
            collective_id=0, has_side_effects=True, vmem_limit_bytes=56 * 1024 * 1024
        ),
        name="attention",
    )(queries, out_grad, key_vectors, value_vectors, block_order)


def solution(mesh, split=SPLIT):
    rows = P("ctx", "head", None)
    return jax.shard_map(
        functools.partial(shards, split),
        mesh=mesh,
        in_specs=(rows, rows, rows, rows, P()),
        out_specs=(rows,) * 4,
        check_vma=False,
    )
```

time: 442 us -> 68.2 us (0.15)
  waiting for transfers between devices: 190 us -> 0 us
  blocking collectives: 134 us -> 0 us
  Pallas kernels: 0 us -> 63.7 us
  matrix products: 48.8 us -> 0 us
  starting transfers between devices: 24.4 us -> 0 us
  local copies, waits for them, and re-layouts: 26 us -> 3.5 us
  between operations: 14.1 us -> 0.65 us
    all_gather x4 -> x0, waiting for transfers between devices: 177 us -> none  [the longest x1 91 us: shards(): lax.all_gather(value_rows, 'ctx', axis=0, tiled=True)]
    all_gather x2 -> x0, blocking collectives: 97.4 us -> none  [the longest x1 49.9 us: shards(): lax.all_gather(log_cols, 'ctx', axis=0, tiled=True)]
    pallas_call x0 -> x1, Pallas kernels: none -> 63.7 us  [shards(): pl.pallas_call(functools.partial(kernel, split), out_shape=tuple((jax.Sha...]
    dot_general x13 -> x0, matrix products: 48.8 us -> none  [the longest x6 21.6 us: contract_rows(): lax.dot_general(left_side, right_side, (((1,), (1,)), ((), ())), preferre...]
    all_to_all x3 -> x0, blocking collectives: 36.3 us -> none  [the longest x1 17.2 us: shards(): lax.all_to_all(widen(key_vectors), 'head', split_axis=2, concat_axis=1, t...]
    all_to_all x5 -> x0, starting transfers between devices: 24 us -> none  [the longest x1 6.26 us: shards(): lax.all_to_all(query_heads.astype(jnp.bfloat16), 'head', split_axis=1, co...]
    all_to_all x5 -> x0, waiting for transfers between devices: 12.7 us -> none  [the longest x1 6.1 us: shards(): lax.all_to_all(out_grad, 'head', split_axis=2, concat_axis=1, tiled=True)]
    all_to_all x6 -> x0, local copies, waits for them, and re-layouts: 8.04 us -> none  [the longest x1 1.69 us: shards(): lax.all_to_all(widen(key_vectors), 'head', split_axis=2, concat_axis=1, t...]
  transfers between devices with their start and end apart: 9 -> 0, of which waited for: 7 -> 0; matrix products, arithmetic and copies ran while one was open for 16% -> 0% of each run, Pallas kernels for 0% -> 0%
where the time goes in v1:
time: 68.2 us; the launch traced here: 67.9 us
  Pallas kernels  63.7 us (93%)
  local copies, waits for them, and re-layouts  3.5 us (5%)
    pallas_call x1, Pallas kernels, shards(): pl.pallas_call(functools.partial(kernel, split), out_shape=tuple((jax.Sha...  63.7 us
    unnamed x10, local copies, waits for them, and re-layouts  3.5 us

profile of v1, /device:TPU:1, one launch (start us, length us, event | category | flops | bytes accessed | tf_op | source)
XLA Modules:
  0.0 67.9 jit_solution(10233709424589129496)
XLA Ops:
  0.6 63.7 %attention.1 = (bf16[2,8,2048]{2,1,0:T(8,128)(2,1)}, bf16[2,8,2048]{2,1,0:T(8,128)(2,1)}, bf16[2,8,256]{2,1,0:T(8,128)(2,1)}, bf16[2,8,256]{2,1,0:T(8,128)(2,1)}) custom-call(bf16[2,8,2048]{2,1,0:T(8,128)(2,1)} %query_ref.1, bf16[2,8,2048]{2,1,0:T(8,128)(2,1)} %grad_ref.1, bf16[2,8,256]{2,1,0:T(8,128)(2,1)} %key_ref.1, bf16[2,8,256]{2,1,0:T(8,128)(2,1)} %value_ref.1, ...), custom_call_target="tpu_custom_call" | custom-call | tf_op jit(solution)/shard_map/attention/pallas_call | solution.py:419
  64.4 0.0 copy-start
  64.4 1.5 %copy.13 = bf16[2,8,2048]{2,1,0:T(8,128)(2,1)} copy(bf16[2,8,2048]{2,1,0:T(8,128)(2,1)} %get-tuple-element.8) | data formatting | bytes 131072
  65.9 0.0 copy-done
  65.9 0.0 copy-start.2
  65.9 0.6 copy.14
  66.5 0.1 copy-done.2
  66.6 0.0 copy-start.1
  66.6 0.6 copy.15
  67.2 0.1 copy-done.1
  67.3 0.6 copy.16
Async XLA Ops:
  64.4 1.5 %copy-start = (bf16[2,8,2048]{2,1,0:T(8,128)(2,1)S(1)}, bf16[2,8,2048]{2,1,0:T(8,128)(2,1)}, u32[]{:S(2)}) copy-start(bf16[2,8,2048]{2,1,0:T(8,128)(2,1)} %get-tuple-element.9) | copy-start | bytes 196612
  65.9 0.7 %copy-start.2 = (bf16[2,8,256]{2,1,0:T(8,128)(2,1)S(1)}, bf16[2,8,256]{2,1,0:T(8,128)(2,1)}, u32[]{:S(2)}) copy-start(bf16[2,8,256]{2,1,0:T(8,128)(2,1)} %get-tuple-element.10) | copy-start | bytes 24580
  66.6 0.7 %copy-start.1 = (bf16[2,8,256]{2,1,0:T(8,128)(2,1)S(1)}, bf16[2,8,256]{2,1,0:T(8,128)(2,1)}, u32[]{:S(2)}) copy-start(bf16[2,8,256]{2,1,0:T(8,128)(2,1)} %get-tuple-element.11) | copy-start | bytes 24580

commit v2 on v1

v2 whole, which is shorter than its diff:
```python
import functools
import math

import jax
import jax.numpy as jnp
from jax import lax
from jax.experimental import pallas as pl
from jax.experimental.pallas import tpu as pltpu
from jax.sharding import PartitionSpec as P

HD = 128
GROUP = 8
ROWS = 8
LOWEST = -1e30
MESH = pl.DeviceIdType.MESH
F32 = jnp.float32
BF16 = jnp.bfloat16

SPLIT = dict(x=4, z_lo=4, y=8, z_hi=2)


def matmul(left_side, right_side):
    return lax.dot_general(
        left_side, right_side, (((1,), (0,)), ((), ())), preferred_element_type=F32
    )


def kernel(
    split,
    query_ref, grad_ref, key_ref, value_ref, order_ref,
    attended_out, query_out, key_out, value_out,
    query_all, grad_all, key_all, value_all, value_stage,
    query_rows, grad_rows, query_cols, grad_cols, key_cols, value_cols,
    key_pos, exps, grad_weights,
    max_rows, sum_rows, dot_rows, ratio_rows, delta_row, stat_all,
    attended_acc, query_acc, out_part, out_in, pair_send, pair_in,
    kv_part, sibling_in, key_send, key_in, value_send, value_in,
    key_last, key_home, value_last, value_home,
    q_ss, q_rs, kz_ss, kz_rs, ky_ss, ky_rs, vy_ss, vy_rs, vz_ss, vz_rs,
    sk_ss, sk_rs, sv_ss, sv_rs, stat_ss, stat_rs, dsib_ss, dsib_rs,
    dky_ss, dky_rs, dkz_ss, dkz_rs, dvz_ss, dvz_rs, dvy_ss, dvy_rs,
    ox_ss, ox_rs, oz_ss, oz_rs, local_sem,
):
    xs, zls, ys, zhs = split["x"], split["z_lo"], split["y"], split["z_hi"]
    zs, srcs = zls * zhs, 2 * xs
    toks = srcs * 2 * ROWS
    cols = GROUP * toks
    keys = 2 * zs * 2 * ROWS
    width = GROUP * HD
    block_len = xs * zls * ROWS
    step = min(256, cols)
    half_ys = ys // 2
    scaling = 1.0 / math.sqrt(HD)
    exp_scale = scaling / math.log(2.0)

    head, ctx = lax.axis_index("head"), lax.axis_index("ctx")
    x, zl = lax.div(head, zls), lax.rem(head, zls)
    core = lax.rem(ctx, 2)
    zh = lax.rem(lax.div(ctx, 2), zhs)
    y = lax.div(ctx, 2 * zhs)
    z = zh * zls + zl
    parity = lax.rem(zl, 2)
    me, mate = x * 2 + parity, x * 2 + 1 - parity

    def at(x_to, y_to, z_to, core_to):
        zh_to, zl_to = lax.div(z_to, zls), lax.rem(z_to, zls)
        return {"head": x_to * zls + zl_to, "ctx": (y_to * zhs + zh_to) * 2 + core_to}

    def at_x(x_to):
        return at(x_to, y, z, core)

    def at_y(y_to):
        return at(x, y_to, z, core)

    def at_z(z_to):
        return at(x, y, z_to, core)

    sibling = at(x, y, z, 1 - core)
    mate_device = at_z(z + 1 - 2 * parity)

    def remote(src, dst, send, recv, device):
        return pltpu.make_async_remote_copy(
            src_ref=src, dst_ref=dst, send_sem=send, recv_sem=recv,
            device_id=device, device_id_type=MESH,
        )

    def nearest(own, order, size):
        odd = lax.rem(order, 2)
        return lax.rem(
            own + odd * (size - lax.div(order + 1, 2)) + (1 - odd) * lax.div(order, 2), size
        )

    def y_of(order):
        return nearest(y, order, ys)

    def z_of(order):
        return nearest(z, order, zs)

    def head_lanes(index, size):
        return pl.ds(pl.multiple_of(index * size, HD), size)

    barrier = pltpu.get_barrier_semaphore()
    greeted = [sibling]
    greeted += [at_x(lax.rem(x + hop, xs)) for hop in range(1, xs)]
    greeted += [at_y(lax.rem(y + hop, ys)) for hop in range(1, ys)]
    greeted += [at_z(lax.rem(z + hop, zs)) for hop in range(1, zs)]
    for device in greeted:
        pl.semaphore_signal(barrier, inc=1, device_id=device, device_id_type=MESH)
    pl.semaphore_wait(barrier, len(greeted))

    def key_z(peer, slot):
        return remote(
            key_ref.at[:, :, head_lanes(lax.rem(peer, 2), HD)], key_all.at[y, core, slot],
            kz_ss.at[peer], kz_rs.at[slot], at_z(peer),
        )

    def value_y(peer, slot):
        return remote(
            value_ref, value_stage.at[slot], vy_ss.at[peer], vy_rs.at[slot], at_y(peer)
        )

    query_refs = ((query_ref, query_all), (grad_ref, grad_all))

    def query_pair(part, slot):
        ref, dst = query_refs[part]
        return remote(
            ref.at[:, :, head_lanes(1 - parity, width)], dst.at[slot],
            q_ss.at[part, x], q_rs.at[part, slot], mate_device,
        )

    def query_own(part, x_to, slot):
        ref, dst = query_refs[part]
        return remote(
            ref.at[:, :, head_lanes(parity, width)], dst.at[slot],
            q_ss.at[part, x_to], q_rs.at[part, slot], at_x(x_to),
        )

    def query_mate(part, x_to, slot):
        dst = query_refs[part][1]
        return remote(
            dst.at[mate], dst.at[slot],
            q_ss.at[part, xs + x_to], q_rs.at[part, slot], at_x(x_to),
        )

    for order in range(1, zs):
        key_z(z_of(order), z).start()
    for order in range(1, ys):
        value_y(y_of(order), y).start()
    for part in range(2):
        query_pair(part, me).start()
    for part in range(2):
        for hop in range(1, xs):
            query_own(part, lax.rem(x + hop, xs), me).start()
    own = [
        pltpu.make_async_copy(
            key_ref.at[:, :, head_lanes(parity, HD)], key_all.at[y, core, z], local_sem.at[0]
        ),
        pltpu.make_async_copy(value_ref, value_stage.at[y], local_sem.at[1]),
    ]
    own += [
        pltpu.make_async_copy(
            ref.at[:, :, head_lanes(parity, width)], dst.at[me], local_sem.at[2 + part]
        )
        for part, (ref, dst) in enumerate(query_refs)
    ]
    for copy in own:
        copy.start()

    row_of = lax.broadcasted_iota(jnp.int32, (ROWS, toks), 0)

    def fill_positions(y_at, carry):
        for core_at in range(2):
            for z_at in range(zs):
                for half in range(2):
                    block = ((y_at * zhs + z_at // zls) * 2 + core_at) * 2 + half
                    first = order_ref[block] * block_len + (x * zls + z_at % zls) * ROWS
                    group = (core_at * zs + z_at) * 2 + half
                    key_pos[y_at, group * ROWS:(group + 1) * ROWS, :] = row_of + first
        return carry

    lax.fori_loop(0, ys, fill_positions, 0)
    token = lax.broadcasted_iota(jnp.int32, (1, toks), 1)
    half_of = lax.rem(lax.div(token, ROWS), 2)
    pair_of = lax.rem(lax.div(token, 2 * ROWS), 2)
    x_of = lax.div(token, 4 * ROWS)
    block_pos = jnp.where(half_of == 0, order_ref[ctx * 2], order_ref[ctx * 2 + 1])
    query_pos = (
        block_pos * block_len
        + (x_of * zls + (zl - parity) + pair_of) * ROWS
        + lax.rem(token, ROWS)
    )
    attended_acc[...] = jnp.zeros_like(attended_acc)
    query_acc[...] = jnp.zeros_like(query_acc)

    def key_y(peer, slot):
        return remote(
            key_all.at[slot, core], key_all.at[slot, core],
            ky_ss.at[peer], ky_rs.at[slot], at_y(peer),
        )

    def value_z(peer, slot):
        return remote(
            value_stage.at[:, :, :, head_lanes(lax.rem(peer, 2), HD)],
            value_all.at[:, core, slot], vz_ss.at[peer], vz_rs.at[slot], at_z(peer),
        )

    def key_sibling(y_at, core_at):
        ref = key_all.at[y_at, core_at]
        return remote(ref, ref, sk_ss.at[y_at], sk_rs.at[y_at], sibling)

    def value_sibling(z_at, core_at):
        ref = value_all.at[:, core_at, z_at]
        return remote(ref, ref, sv_ss.at[z_at], sv_rs.at[z_at], sibling)

    for copy in own:
        copy.wait()
    for order in range(1, zs):
        key_z(z, z_of(order)).wait_recv()
    for order in range(1, ys):
        key_y(y_of(order), y).start()
    key_sibling(y, core).start()
    for order in range(1, ys):
        value_y(y, y_of(order)).wait_recv()
    for order in range(1, zs):
        value_z(z_of(order), z).start()
    own_value = pltpu.make_async_copy(
        value_stage.at[:, :, :, head_lanes(parity, HD)], value_all.at[:, core, z],
        local_sem.at[4],
    )
    own_value.start()
    for part in range(2):
        query_pair(part, mate).wait_recv()
        for hop in range(1, xs):
            query_mate(part, lax.rem(x + hop, xs), mate).start()
    own_value.wait()
    value_sibling(z, core).start()
    for part in range(2):
        for hop in range(1, xs):
            other = lax.rem(x + hop, xs)
            query_own(part, x, other * 2 + parity).wait_recv()
            query_mate(part, x, other * 2 + 1 - parity).wait_recv()
    for head_at in range(GROUP):
        lanes = slice(head_at * HD, (head_at + 1) * HD)
        rows = slice(head_at * toks, (head_at + 1) * toks)
        for src, by_row, by_col in (
            (query_all, query_rows, query_cols), (grad_all, grad_rows, grad_cols)
        ):
            tile = src[:, :, :, lanes].astype(F32).reshape(toks, HD)
            by_row[rows, :] = tile.astype(BF16)
            by_col[:, rows] = tile.T.astype(BF16)

    def pass_key(order):
        y_at = y_of(order)
        key_y(y, y_at).wait_recv()
        key_sibling(y_at, core).start()

    def pass_value(order):
        z_at = z_of(order)
        value_z(z, z_at).wait_recv()
        value_sibling(z_at, core).start()

    def score(order, carry):
        @pl.when(order + 1 < ys)
        def _():
            pass_key(order + 1)

        @pl.when(order + 1 < zs)
        def _():
            pass_value(order + 1)

        y_at = y_of(order)
        key_sibling(y_at, 1 - core).wait_recv()
        key_wide = key_all[y_at].astype(F32).reshape(keys, HD)
        key_cols[y_at] = key_wide.T.astype(BF16)
        key_tile = key_wide.astype(BF16)
        allowed = jnp.concatenate([key_pos[y_at]] * (step // toks), axis=1) <= jnp.concatenate(
            [query_pos] * (step // toks), axis=1
        )
        for first in range(0, cols, step):
            lanes = slice(first, first + step)
            scores = jnp.where(allowed, matmul(key_tile, query_cols[:, lanes]), LOWEST)
            top = jnp.max(scores, axis=0, keepdims=True)
            exp_tile = jnp.exp2((scores - top) * exp_scale)
            exps[y_at, :, lanes] = exp_tile
            max_rows[pl.ds(y_at, 1), lanes] = top
            sum_rows[pl.ds(y_at, 1), lanes] = jnp.sum(exp_tile, axis=0, keepdims=True)
        return carry

    lax.fori_loop(0, ys, score, 0)
    for order in range(ys + 1, zs):
        pass_value(order)
    for order in range(zs):
        value_sibling(z_of(order), 1 - core).wait_recv()

    def weigh(y_at, carry):
        value_wide = value_all[y_at].astype(F32).reshape(keys, HD)
        value_cols[y_at] = value_wide.T.astype(BF16)
        value_tile = value_wide.astype(BF16)
        for first in range(0, cols, step):
            lanes = slice(first, first + step)
            weight_grad = matmul(value_tile, grad_cols[:, lanes])
            grad_weights[y_at, :, lanes] = weight_grad
            dot_rows[pl.ds(y_at, 1), lanes] = jnp.sum(
                exps[y_at, :, lanes] * weight_grad, axis=0, keepdims=True
            )
        return carry

    lax.fori_loop(0, ys, weigh, 0)

    top = jnp.max(max_rows[...], axis=0, keepdims=True)
    factor = jnp.exp2((max_rows[...] - top) * exp_scale)
    for index, row in enumerate((
        top,
        jnp.sum(sum_rows[...] * factor, axis=0, keepdims=True),
        jnp.sum(dot_rows[...] * factor, axis=0, keepdims=True),
    )):
        for head_at in range(GROUP):
            stat_all[x, index, head_at:head_at + 1, :] = row[
                :, head_at * toks:(head_at + 1) * toks
            ]

    def stat_copy(peer, slot):
        return remote(
            stat_all.at[slot], stat_all.at[slot], stat_ss.at[peer], stat_rs.at[slot], at_x(peer)
        )

    for hop in range(1, xs):
        stat_copy(lax.rem(x + hop, xs), x).start()
    for hop in range(1, xs):
        stat_copy(x, lax.rem(x + hop, xs)).wait_recv()
    tops = [stat_all[x_at, 0] for x_at in range(xs)]
    top = functools.reduce(jnp.maximum, tops)
    factors = [jnp.exp2((part - top) * exp_scale) for part in tops]
    total = sum(stat_all[x_at, 1] * factors[x_at] for x_at in range(xs))
    inverse = 1.0 / total
    delta = sum(stat_all[x_at, 2] * factors[x_at] for x_at in range(xs)) * inverse
    for head_at in range(GROUP):
        lanes = slice(head_at * toks, (head_at + 1) * toks)
        row = slice(head_at, head_at + 1)
        delta_row[:, lanes] = delta[row]
        ratio_rows[:, lanes] = (
            jnp.exp2((max_rows[:, lanes] - top[row]) * exp_scale) * inverse[row]
        )

    def dsib_copy(order, core_at):
        return remote(
            kv_part.at[order, core_at], sibling_in.at[order],
            dsib_ss.at[order], dsib_rs.at[order], sibling,
        )

    def dkey_y(order):
        return remote(
            key_send.at[order], key_in.at[order],
            dky_ss.at[order], dky_rs.at[order], at_y(y_of(order)),
        )

    def dvalue_z(batch, peer, slot):
        orders = pl.ds(batch * half_ys, half_ys)
        return remote(
            value_send.at[peer, orders], value_in.at[slot, orders],
            dvz_ss.at[batch, peer], dvz_rs.at[batch, slot], at_z(peer),
        )

    def add_sibling(order):
        dsib_copy(order, 1 - core).wait_recv()
        key_send[order] = (
            kv_part[order, core, 0].astype(F32) + sibling_in[order, 0].astype(F32)
        ).astype(BF16)
        value_send[:, order] = (
            kv_part[order, core, 1].astype(F32) + sibling_in[order, 1].astype(F32)
        ).astype(BF16)

    def backward(turn, carry):
        order = ys - 1 - turn
        y_at = y_of(order)
        key_sum = jnp.zeros((keys, HD), F32)
        value_sum = jnp.zeros((keys, HD), F32)
        for first in range(0, cols, step):
            lanes = slice(first, first + step)
            probs = exps[y_at, :, lanes] * ratio_rows[pl.ds(y_at, 1), lanes]
            weights = probs.astype(BF16)
            grad_scores = (
                probs * (grad_weights[y_at, :, lanes] - delta_row[:, lanes])
            ).astype(BF16)
            attended_acc[:, lanes] += matmul(value_cols[y_at], weights)
            query_acc[:, lanes] += matmul(key_cols[y_at], grad_scores)
            value_sum += matmul(weights, grad_rows[lanes, :])
            key_sum += matmul(grad_scores, query_rows[lanes, :])
        shape = (2, zs, 2, ROWS, HD)
        kv_part[order, :, 0] = (key_sum * scaling).reshape(shape).astype(BF16)
        kv_part[order, :, 1] = value_sum.reshape(shape).astype(BF16)
        dsib_copy(order, 1 - core).start()

        @pl.when(turn >= 1)
        def _():
            add_sibling(order + 1)
            dkey_y(order + 1).start()

        @pl.when(order + 1 == half_ys)
        def _():
            for near in range(1, zs):
                dvalue_z(1, z_of(near), z).start()

        return carry

    lax.fori_loop(0, ys, backward, 0)

    for head_at in range(GROUP):
        lanes = slice(head_at * HD, (head_at + 1) * HD)
        rows = slice(head_at * toks, (head_at + 1) * toks)
        shape = (xs, 2, 2, ROWS, HD)
        out_part[:, :, 0, :, :, lanes] = attended_acc[:, rows].T.reshape(shape).astype(BF16)
        out_part[:, :, 1, :, :, lanes] = (
            (query_acc[:, rows] * scaling).T.reshape(shape).astype(BF16)
        )

    def out_x(peer, slot):
        return remote(
            out_part.at[peer], out_in.at[slot], ox_ss.at[peer], ox_rs.at[slot], at_x(peer)
        )

    for hop in range(1, xs):
        out_x(lax.rem(x + hop, xs), x).start()
    add_sibling(0)
    for near in range(1, zs):
        dvalue_z(0, z_of(near), z).start()
    out_in[x] = out_part[x]
    value_in[z] = value_send[z]

    total_key = key_send[0].astype(F32)
    for order in range(1, ys):
        dkey_y(order).wait_recv()
        total_key += key_in[order].astype(F32)
    key_last[...] = total_key.astype(BF16)

    def dkey_z(peer, slot):
        return remote(
            key_last.at[peer], key_home.at[slot], dkz_ss.at[peer], dkz_rs.at[slot], at_z(peer)
        )

    def dvalue_y(order):
        return remote(
            value_last.at[order], value_home.at[order],
            dvy_ss.at[order], dvy_rs.at[order], at_y(y_of(order)),
        )

    for near in range(1, zs):
        dkey_z(z_of(near), z).start()
    key_home[z] = key_last[z]
    for near in range(1, zs):
        for batch in range(2):
            dvalue_z(batch, z, z_of(near)).wait_recv()
    for half in range(2):
        value_last[:, half] = sum(
            value_in[z_at].astype(F32) for z_at in range(half, zs, 2)
        ).astype(BF16)
    for order in range(1, ys):
        dvalue_y(order).start()
    value_home[0] = value_last[0]

    for hop in range(1, xs):
        out_x(x, lax.rem(x + hop, xs)).wait_recv()
    pair_send[...] = sum(
        out_in[x_at, 1 - parity].astype(F32) for x_at in range(xs)
    ).astype(BF16)
    pair_copy = remote(pair_send, pair_in, oz_ss.at[0], oz_rs.at[0], mate_device)
    pair_copy.start()
    mine = sum(out_in[x_at, parity].astype(F32) for x_at in range(xs)).astype(BF16)
    for part, out in enumerate((attended_out, query_out)):
        out[:, :, head_lanes(parity, width)] = mine[part]

    for near in range(1, zs):
        dkey_z(z, z_of(near)).wait_recv()
    for half in range(2):
        key_out[:, :, half * HD:(half + 1) * HD] = sum(
            key_home[z_at].astype(F32) for z_at in range(half, zs, 2)
        ).astype(BF16)
    for order in range(1, ys):
        dvalue_y(order).wait_recv()
    for half in range(2):
        value_out[:, :, half * HD:(half + 1) * HD] = sum(
            value_home[order, half].astype(F32) for order in range(ys)
        ).astype(BF16)
    pair_copy.wait_recv()
    for part, out in enumerate((attended_out, query_out)):
        out[:, :, head_lanes(1 - parity, width)] = pair_in[part]

    for order in range(zs):
        peer = z_of(order)
        value_sibling(peer, core).wait_send()
        if order:
            key_z(peer, z).wait_send()
            value_z(peer, z).wait_send()
            dkey_z(peer, z).wait_send()
            for batch in range(2):
                dvalue_z(batch, peer, z).wait_send()
    for order in range(ys):
        peer = y_of(order)
        key_sibling(peer, core).wait_send()
        dsib_copy(order, 1 - core).wait_send()
        if order:
            value_y(peer, y).wait_send()
            key_y(peer, y).wait_send()
            dkey_y(order).wait_send()
            dvalue_y(order).wait_send()
    for hop in range(1, xs):
        peer = lax.rem(x + hop, xs)
        for part in range(2):
            query_own(part, peer, me).wait_send()
            query_mate(part, peer, mate).wait_send()
        stat_copy(peer, x).wait_send()
        out_x(peer, x).wait_send()
    for part in range(2):
        query_pair(part, me).wait_send()
    pair_copy.wait_send()


def finish(*refs):
    for src, dst in zip(refs[:4], refs[4:]):
        dst[...] = src[...]


def shards(split, queries, key_vectors, value_vectors, out_grad, block_order):
    xs, zls, ys, zhs = split["x"], split["z_lo"], split["y"], split["z_hi"]
    zs, srcs = zls * zhs, 2 * xs
    toks = srcs * 2 * ROWS
    cols = GROUP * toks
    keys = 2 * zs * 2 * ROWS
    width = GROUP * HD
    vmem = pltpu.VMEM
    dma = pltpu.SemaphoreType.DMA
    tile = (2, ROWS, HD)
    whole = pl.BlockSpec(memory_space=pltpu.VMEM)
    results = tuple(
        jax.ShapeDtypeStruct(a.shape, BF16)
        for a in (queries, queries, key_vectors, value_vectors)
    )
    partial_sums = pl.pallas_call(
        functools.partial(kernel, split),
        out_shape=results,
        in_specs=[whole] * 4 + [pl.BlockSpec(memory_space=pltpu.SMEM)],
        out_specs=(whole,) * 4,
        scratch_shapes=[
            vmem((srcs, 2, ROWS, width), BF16), vmem((srcs, 2, ROWS, width), BF16),
            vmem((ys, 2, zs) + tile, BF16), vmem((ys, 2, zs) + tile, BF16),
            vmem((ys,) + value_vectors.shape, BF16),
            vmem((cols, HD), BF16), vmem((cols, HD), BF16),
            vmem((HD, cols), BF16), vmem((HD, cols), BF16),
            vmem((ys, HD, keys), BF16), vmem((ys, HD, keys), BF16),
            vmem((ys, keys, toks), jnp.int32),
            vmem((ys, keys, cols), F32), vmem((ys, keys, cols), F32),
            vmem((ys, cols), F32), vmem((ys, cols), F32), vmem((ys, cols), F32),
            vmem((ys, cols), F32), vmem((1, cols), F32), vmem((xs, 3, GROUP, toks), F32),
            vmem((HD, cols), F32), vmem((HD, cols), F32),
            vmem((xs, 2, 2, 2, ROWS, width), BF16), vmem((xs, 2, 2, 2, ROWS, width), BF16),
            vmem((2, 2, ROWS, width), BF16), vmem((2, 2, ROWS, width), BF16),
            vmem((ys, 2, 2, zs) + tile, BF16), vmem((ys, 2, zs) + tile, BF16),
            vmem((ys, zs) + tile, BF16), vmem((ys, zs) + tile, BF16),
            vmem((zs, ys) + tile, BF16), vmem((zs, ys) + tile, BF16),
            vmem((zs,) + tile, BF16), vmem((zs,) + tile, BF16),
            vmem((ys, 2) + tile, BF16), vmem((ys, 2) + tile, BF16),
            dma((2, 2 * xs)), dma((2, srcs)), dma((zs,)), dma((zs,)), dma((ys,)), dma((ys,)),
            dma((ys,)), dma((ys,)), dma((zs,)), dma((zs,)),
            dma((ys,)), dma((ys,)), dma((zs,)), dma((zs,)), dma((xs,)), dma((xs,)),
            dma((ys,)), dma((ys,)),
            dma((ys,)), dma((ys,)), dma((zs,)), dma((zs,)),
            dma((2, zs)), dma((2, zs)), dma((ys,)), dma((ys,)),
            dma((xs,)), dma((xs,)), dma((1,)), dma((1,)), dma((5,)),
        ],
        compiler_params=pltpu.CompilerParams(
            collective_id=0, has_side_effects=True, vmem_limit_bytes=56 * 1024 * 1024
        ),
        name="attention",
    )(queries, out_grad, key_vectors, value_vectors, block_order)
    return pl.pallas_call(
        finish, out_shape=results, in_specs=[whole] * 4, out_specs=(whole,) * 4, name="finish"
    )(*partial_sums)


def solution(mesh, split=SPLIT):
    rows = P("ctx", "head", None)
    return jax.shard_map(
        functools.partial(shards, split),
        mesh=mesh,
        in_specs=(rows, rows, rows, rows, P()),
        out_specs=(rows,) * 4,
        check_vma=False,
    )
```

time: 68.2 us -> 61.2 us (0.90)
  local copies, waits for them, and re-layouts: 3.5 us -> 0 us
  Pallas kernels: 63.7 us -> 60.4 us
    unnamed x10 -> x0, local copies, waits for them, and re-layouts: 3.5 us -> none
    pallas_call x1 -> x2, Pallas kernels: 63.7 us -> 60.4 us  [the longest x1 58.9 us: shards(): pl.pallas_call(functools.partial(kernel, split), out_shape=results, in_sp...]
where the time goes in v2:
time: 61.2 us; the launch traced here: 61 us
  Pallas kernels  60.4 us (99%)
  between operations  0.64 us (1%)
    pallas_call x1, Pallas kernels, shards(): pl.pallas_call(functools.partial(kernel, split), out_shape=results, in_sp...  58.9 us
    pallas_call x1, Pallas kernels, shards(): pl.pallas_call(finish, out_shape=results, in_specs=[whole] * 4, out_specs...  1.54 us

profile of v2, /device:TPU:1, one launch (start us, length us, event | category | flops | bytes accessed | tf_op | source)
XLA Modules:
  0.0 61.0 jit_solution(9437265698826529169)
XLA Ops:
  0.6 58.9 %attention.1 = (bf16[2,8,2048]{2,1,0:T(8,128)(2,1)}, bf16[2,8,2048]{2,1,0:T(8,128)(2,1)}, bf16[2,8,256]{2,1,0:T(8,128)(2,1)}, bf16[2,8,256]{2,1,0:T(8,128)(2,1)}) custom-call(bf16[2,8,2048]{2,1,0:T(8,128)(2,1)} %query_ref.1, bf16[2,8,2048]{2,1,0:T(8,128)(2,1)} %grad_ref.1, bf16[2,8,256]{2,1,0:T(8,128)(2,1)} %key_ref.1, bf16[2,8,256]{2,1,0:T(8,128)(2,1)} %value_ref.1, ...), custom_call_target="tpu_custom_call" | custom-call | tf_op jit(solution)/shard_map/attention/pallas_call | solution.py:538
  59.5 1.5 %finish.1 = (bf16[2,8,2048]{2,1,0:T(8,128)(2,1)}, bf16[2,8,2048]{2,1,0:T(8,128)(2,1)}, bf16[2,8,256]{2,1,0:T(8,128)(2,1)}, bf16[2,8,256]{2,1,0:T(8,128)(2,1)}) custom-call(bf16[2,8,2048]{2,1,0:T(8,128)(2,1)} %get-tuple-element.8.refs_0_, bf16[2,8,2048]{2,1,0:T(8,128)(2,1)} %get-tuple-element.9.refs_1_, bf16[2,8,256]{2,1,0:T(8,128)(2,1)} %get-tuple-element.10.refs_2_, ...), custom_call_target="tpu_custom_call" | custom-call | tf_op jit(solution)/shard_map/finish/pallas_call | solution.py:575

commit v3 on v2

--- a/solution.py
+++ b/solution.py
@@ -32,7 +32,7 @@
     query_all, grad_all, key_all, value_all, value_stage,
     query_rows, grad_rows, query_cols, grad_cols, key_cols, value_cols,
     key_pos, exps, grad_weights,
-    max_rows, sum_rows, dot_rows, ratio_rows, delta_row, stat_all,
+    max_rows, sum_rows, dot_rows, ratio_rows, delta_row, scale_row, stat_all,
     attended_acc, query_acc, out_part, out_in, pair_send, pair_in,
     kv_part, sibling_in, key_send, key_in, value_send, value_in,
     key_last, key_home, value_last, value_home,
@@ -49,7 +49,6 @@
     width = GROUP * HD
     block_len = xs * zls * ROWS
     step = min(256, cols)
-    half_ys = ys // 2
     scaling = 1.0 / math.sqrt(HD)
     exp_scale = scaling / math.log(2.0)
 
@@ -309,6 +308,8 @@
 
     top = jnp.max(max_rows[...], axis=0, keepdims=True)
     factor = jnp.exp2((max_rows[...] - top) * exp_scale)
+    ratio_rows[...] = factor
+    scale_row[...] = top
     for index, row in enumerate((
         top,
         jnp.sum(sum_rows[...] * factor, axis=0, keepdims=True),
@@ -326,8 +327,37 @@
 
     for hop in range(1, xs):
         stat_copy(lax.rem(x + hop, xs), x).start()
+
+    for order in range(zs):
+        peer = z_of(order)
+        value_sibling(peer, core).wait_send()
+        if order:
+            key_z(peer, z).wait_send()
+            value_z(peer, z).wait_send()
+    for order in range(ys):
+        peer = y_of(order)
+        key_sibling(peer, core).wait_send()
+        if order:
+            value_y(peer, y).wait_send()
+            key_y(peer, y).wait_send()
+    for part in range(2):
+        query_pair(part, me).wait_send()
+        for hop in range(1, xs):
+            query_own(part, lax.rem(x + hop, xs), me).wait_send()
+            query_mate(part, lax.rem(x + hop, xs), mate).wait_send()
+
+    def attend(y_at, carry):
+        for first in range(0, cols, step):
+            lanes = slice(first, first + step)
+            weights = exps[y_at, :, lanes] * ratio_rows[pl.ds(y_at, 1), lanes]
+            attended_acc[:, lanes] += matmul(value_cols[y_at], weights.astype(BF16))
+        return carry
+
+    lax.fori_loop(0, ys, attend, 0)
+
     for hop in range(1, xs):
         stat_copy(x, lax.rem(x + hop, xs)).wait_recv()
+        stat_copy(lax.rem(x + hop, xs), x).wait_send()
     tops = [stat_all[x_at, 0] for x_at in range(xs)]
     top = functools.reduce(jnp.maximum, tops)
     factors = [jnp.exp2((part - top) * exp_scale) for part in tops]
@@ -338,10 +368,48 @@
         lanes = slice(head_at * toks, (head_at + 1) * toks)
         row = slice(head_at, head_at + 1)
         delta_row[:, lanes] = delta[row]
+        scale_row[:, lanes] = (
+            jnp.exp2((scale_row[:, lanes] - top[row]) * exp_scale) * inverse[row]
+        )
         ratio_rows[:, lanes] = (
             jnp.exp2((max_rows[:, lanes] - top[row]) * exp_scale) * inverse[row]
         )
 
+    def out_x(part, peer, slot):
+        return remote(
+            out_part.at[part, peer], out_in.at[part, slot],
+            ox_ss.at[part, peer], ox_rs.at[part, slot], at_x(peer),
+        )
+
+    def out_pair(part):
+        return remote(
+            pair_send.at[part], pair_in.at[part], oz_ss.at[part], oz_rs.at[part], mate_device
+        )
+
+    def send_out(part, acc, scale):
+        for head_at in range(GROUP):
+            lanes = slice(head_at * HD, (head_at + 1) * HD)
+            rows = slice(head_at * toks, (head_at + 1) * toks)
+            out_part[part, :, :, :, :, lanes] = (
+                (acc[:, rows] * scale(rows)).T.reshape(xs, 2, 2, ROWS, HD).astype(BF16)
+            )
+        for hop in range(1, xs):
+            out_x(part, lax.rem(x + hop, xs), x).start()
+        out_in[part, x] = out_part[part, x]
+
+    def add_out(part, out):
+        for hop in range(1, xs):
+            out_x(part, x, lax.rem(x + hop, xs)).wait_recv()
+        pair_send[part] = sum(
+            out_in[part, x_at, 1 - parity].astype(F32) for x_at in range(xs)
+        ).astype(BF16)
+        out_pair(part).start()
+        out[:, :, head_lanes(parity, width)] = sum(
+            out_in[part, x_at, parity].astype(F32) for x_at in range(xs)
+        ).astype(BF16)
+
+    send_out(0, attended_acc, lambda rows: scale_row[:, rows])
+
     def dsib_copy(order, core_at):
         return remote(
             kv_part.at[order, core_at], sibling_in.at[order],
@@ -354,11 +422,15 @@
             dky_ss.at[order], dky_rs.at[order], at_y(y_of(order)),
         )
 
-    def dvalue_z(batch, peer, slot):
-        orders = pl.ds(batch * half_ys, half_ys)
-        return remote(
-            value_send.at[peer, orders], value_in.at[slot, orders],
-            dvz_ss.at[batch, peer], dvz_rs.at[batch, slot], at_z(peer),
+    def dvalue_z(order, peer, slot):
+        return remote(
+            value_send.at[peer, order], value_in.at[slot, order],
+            dvz_ss.at[peer], dvz_rs.at[slot], at_z(peer),
+        )
+
+    def dvalue_all(peer, slot):
+        return remote(
+            value_send.at[peer], value_in.at[slot], dvz_ss.at[peer], dvz_rs.at[slot], at_z(peer)
         )
 
     def add_sibling(order):
@@ -369,6 +441,8 @@
         value_send[:, order] = (
             kv_part[order, core, 1].astype(F32) + sibling_in[order, 1].astype(F32)
         ).astype(BF16)
+        for near in range(1, zs):
+            dvalue_z(order, z_of(near), z).start()
 
     def backward(turn, carry):
         order = ys - 1 - turn
@@ -382,7 +456,6 @@
             grad_scores = (
                 probs * (grad_weights[y_at, :, lanes] - delta_row[:, lanes])
             ).astype(BF16)
-            attended_acc[:, lanes] += matmul(value_cols[y_at], weights)
             query_acc[:, lanes] += matmul(key_cols[y_at], grad_scores)
             value_sum += matmul(weights, grad_rows[lanes, :])
             key_sum += matmul(grad_scores, query_rows[lanes, :])
@@ -396,35 +469,13 @@
             add_sibling(order + 1)
             dkey_y(order + 1).start()
 
-        @pl.when(order + 1 == half_ys)
-        def _():
-            for near in range(1, zs):
-                dvalue_z(1, z_of(near), z).start()
-
         return carry
 
     lax.fori_loop(0, ys, backward, 0)
 
-    for head_at in range(GROUP):
-        lanes = slice(head_at * HD, (head_at + 1) * HD)
-        rows = slice(head_at * toks, (head_at + 1) * toks)
-        shape = (xs, 2, 2, ROWS, HD)
-        out_part[:, :, 0, :, :, lanes] = attended_acc[:, rows].T.reshape(shape).astype(BF16)
-        out_part[:, :, 1, :, :, lanes] = (
-            (query_acc[:, rows] * scaling).T.reshape(shape).astype(BF16)
-        )
-
-    def out_x(peer, slot):
-        return remote(
-            out_part.at[peer], out_in.at[slot], ox_ss.at[peer], ox_rs.at[slot], at_x(peer)
-        )
-
-    for hop in range(1, xs):
-        out_x(lax.rem(x + hop, xs), x).start()
+    send_out(1, query_acc, lambda rows: scaling)
+    add_out(0, attended_out)
     add_sibling(0)
-    for near in range(1, zs):
-        dvalue_z(0, z_of(near), z).start()
-    out_in[x] = out_part[x]
     value_in[z] = value_send[z]
 
     total_key = key_send[0].astype(F32)
@@ -448,8 +499,7 @@
         dkey_z(z_of(near), z).start()
     key_home[z] = key_last[z]
     for near in range(1, zs):
-        for batch in range(2):
-            dvalue_z(batch, z, z_of(near)).wait_recv()
+        dvalue_all(z, z_of(near)).wait_recv()
     for half in range(2):
         value_last[:, half] = sum(
             value_in[z_at].astype(F32) for z_at in range(half, zs, 2)
@@ -458,17 +508,7 @@
         dvalue_y(order).start()
     value_home[0] = value_last[0]
 
-    for hop in range(1, xs):
-        out_x(x, lax.rem(x + hop, xs)).wait_recv()
-    pair_send[...] = sum(
-        out_in[x_at, 1 - parity].astype(F32) for x_at in range(xs)
-    ).astype(BF16)
-    pair_copy = remote(pair_send, pair_in, oz_ss.at[0], oz_rs.at[0], mate_device)
-    pair_copy.start()
-    mine = sum(out_in[x_at, parity].astype(F32) for x_at in range(xs)).astype(BF16)
-    for part, out in enumerate((attended_out, query_out)):
-        out[:, :, head_lanes(parity, width)] = mine[part]
-
+    add_out(1, query_out)
     for near in range(1, zs):
         dkey_z(z, z_of(near)).wait_recv()
     for half in range(2):
@@ -481,38 +521,23 @@
         value_out[:, :, half * HD:(half + 1) * HD] = sum(
             value_home[order, half].astype(F32) for order in range(ys)
         ).astype(BF16)
-    pair_copy.wait_recv()
     for part, out in enumerate((attended_out, query_out)):
+        out_pair(part).wait_recv()
         out[:, :, head_lanes(1 - parity, width)] = pair_in[part]
 
-    for order in range(zs):
+    for order in range(1, zs):
         peer = z_of(order)
-        value_sibling(peer, core).wait_send()
-        if order:
-            key_z(peer, z).wait_send()
-            value_z(peer, z).wait_send()
-            dkey_z(peer, z).wait_send()
-            for batch in range(2):
-                dvalue_z(batch, peer, z).wait_send()
+        dkey_z(peer, z).wait_send()
+        dvalue_all(peer, z).wait_send()
     for order in range(ys):
-        peer = y_of(order)
-        key_sibling(peer, core).wait_send()
         dsib_copy(order, 1 - core).wait_send()
         if order:
-            value_y(peer, y).wait_send()
-            key_y(peer, y).wait_send()
             dkey_y(order).wait_send()
             dvalue_y(order).wait_send()
-    for hop in range(1, xs):
-        peer = lax.rem(x + hop, xs)
-        for part in range(2):
-            query_own(part, peer, me).wait_send()
-            query_mate(part, peer, mate).wait_send()
-        stat_copy(peer, x).wait_send()
-        out_x(peer, x).wait_send()
     for part in range(2):
-        query_pair(part, me).wait_send()
-    pair_copy.wait_send()
+        for hop in range(1, xs):
+            out_x(part, lax.rem(x + hop, xs), x).wait_send()
+        out_pair(part).wait_send()
 
 
 def finish(*refs):
@@ -538,7 +563,8 @@
     partial_sums = pl.pallas_call(
         functools.partial(kernel, split),
         out_shape=results,
-        in_specs=[whole] * 4 + [pl.BlockSpec(memory_space=pltpu.SMEM)],
+        in_specs=[pl.BlockSpec(memory_space=pl.ANY)] * 4
+        + [pl.BlockSpec(memory_space=pltpu.SMEM)],
         out_specs=(whole,) * 4,
         scratch_shapes=[
             vmem((srcs, 2, ROWS, width), BF16), vmem((srcs, 2, ROWS, width), BF16),
@@ -550,9 +576,10 @@
             vmem((ys, keys, toks), jnp.int32),
             vmem((ys, keys, cols), F32), vmem((ys, keys, cols), F32),
             vmem((ys, cols), F32), vmem((ys, cols), F32), vmem((ys, cols), F32),
-            vmem((ys, cols), F32), vmem((1, cols), F32), vmem((xs, 3, GROUP, toks), F32),
+            vmem((ys, cols), F32), vmem((1, cols), F32), vmem((1, cols), F32),
+            vmem((xs, 3, GROUP, toks), F32),
             vmem((HD, cols), F32), vmem((HD, cols), F32),
-            vmem((xs, 2, 2, 2, ROWS, width), BF16), vmem((xs, 2, 2, 2, ROWS, width), BF16),
+            vmem((2, xs, 2, 2, ROWS, width), BF16), vmem((2, xs, 2, 2, ROWS, width), BF16),
             vmem((2, 2, ROWS, width), BF16), vmem((2, 2, ROWS, width), BF16),
             vmem((ys, 2, 2, zs) + tile, BF16), vmem((ys, 2, zs) + tile, BF16),
             vmem((ys, zs) + tile, BF16), vmem((ys, zs) + tile, BF16),
@@ -564,8 +591,8 @@
             dma((ys,)), dma((ys,)), dma((zs,)), dma((zs,)), dma((xs,)), dma((xs,)),
             dma((ys,)), dma((ys,)),
             dma((ys,)), dma((ys,)), dma((zs,)), dma((zs,)),
-            dma((2, zs)), dma((2, zs)), dma((ys,)), dma((ys,)),
-            dma((xs,)), dma((xs,)), dma((1,)), dma((1,)), dma((5,)),
+            dma((zs,)), dma((zs,)), dma((ys,)), dma((ys,)),
+            dma((2, xs)), dma((2, xs)), dma((2,)), dma((2,)), dma((5,)),
         ],
         compiler_params=pltpu.CompilerParams(
             collective_id=0, has_side_effects=True, vmem_limit_bytes=56 * 1024 * 1024

time: 61.2 us -> 58.8 us (0.961)
  Pallas kernels: 60.4 us -> 57.7 us
    pallas_call x1, Pallas kernels: 58.9 us -> 56.2 us  [shards(): pl.pallas_call(functools.partial(kernel, split), out_shape=results, in_sp...]
where the time goes in v3:
time: 58.8 us; the launch traced here: 58.4 us
  Pallas kernels  57.7 us (98%)
  between operations  0.64 us (1%)
    pallas_call x1, Pallas kernels, shards(): pl.pallas_call(functools.partial(kernel, split), out_shape=results, in_sp...  56.2 us
    pallas_call x1, Pallas kernels, shards(): pl.pallas_call(finish, out_shape=results, in_specs=[whole] * 4, out_specs...  1.54 us

profile of v3, /device:TPU:1, one launch (start us, length us, event | category | flops | bytes accessed | tf_op | source)
XLA Modules:
  0.0 58.4 jit_solution(1147010280718900261)
XLA Ops:
  0.6 56.2 %attention.1 = (bf16[2,8,2048]{2,1,0:T(8,128)(2,1)}, bf16[2,8,2048]{2,1,0:T(8,128)(2,1)}, bf16[2,8,256]{2,1,0:T(8,128)(2,1)}, bf16[2,8,256]{2,1,0:T(8,128)(2,1)}) custom-call(bf16[2,8,2048]{2,1,0:T(8,128)(2,1)} %query_ref.1, bf16[2,8,2048]{2,1,0:T(8,128)(2,1)} %grad_ref.1, bf16[2,8,256]{2,1,0:T(8,128)(2,1)} %key_ref.1, bf16[2,8,256]{2,1,0:T(8,128)(2,1)} %value_ref.1, ...), custom_call_target="tpu_custom_call" | custom-call | tf_op jit(solution)/shard_map/attention/pallas_call | solution.py:563
  56.8 1.5 %finish.1 = (bf16[2,8,2048]{2,1,0:T(8,128)(2,1)}, bf16[2,8,2048]{2,1,0:T(8,128)(2,1)}, bf16[2,8,256]{2,1,0:T(8,128)(2,1)}, bf16[2,8,256]{2,1,0:T(8,128)(2,1)}) custom-call(bf16[2,8,2048]{2,1,0:T(8,128)(2,1)} %get-tuple-element.8.refs_0_, bf16[2,8,2048]{2,1,0:T(8,128)(2,1)} %get-tuple-element.9.refs_1_, bf16[2,8,256]{2,1,0:T(8,128)(2,1)} %get-tuple-element.10.refs_2_, ...), custom_call_target="tpu_custom_call" | custom-call | tf_op jit(solution)/shard_map/finish/pallas_call | solution.py:602

commit v4 on v3

--- a/solution.py
+++ b/solution.py
@@ -16,6 +16,8 @@
 F32 = jnp.float32
 BF16 = jnp.bfloat16
 
+AHEAD = 2
+
 SPLIT = dict(x=4, z_lo=4, y=8, z_hi=2)
 
 
@@ -30,9 +32,9 @@
     query_ref, grad_ref, key_ref, value_ref, order_ref,
     attended_out, query_out, key_out, value_out,
     query_all, grad_all, key_all, value_all, value_stage,
-    query_rows, grad_rows, query_cols, grad_cols, key_cols, value_cols,
-    key_pos, exps, grad_weights,
-    max_rows, sum_rows, dot_rows, ratio_rows, delta_row, scale_row, stat_all,
+    query_rows, grad_rows, query_cols, grad_cols, key_cols,
+    key_pos, exps, exps_low, grad_weights,
+    max_rows, sum_rows, ratio_rows, delta_row, scale_row, stat_all,
     attended_acc, query_acc, out_part, out_in, pair_send, pair_in,
     kv_part, sibling_in, key_send, key_in, value_send, value_in,
     key_last, key_home, value_last, value_home,
@@ -141,9 +143,9 @@
             q_ss.at[part, xs + x_to], q_rs.at[part, slot], at_x(x_to),
         )
 
-    for order in range(1, zs):
+    for order in reversed(range(1, zs)):
         key_z(z_of(order), z).start()
-    for order in range(1, ys):
+    for order in reversed(range(1, ys)):
         value_y(y_of(order), y).start()
     for part in range(2):
         query_pair(part, me).start()
@@ -259,13 +261,13 @@
         value_sibling(z_at, core).start()
 
     def score(order, carry):
-        @pl.when(order + 1 < ys)
+        @pl.when(order + AHEAD < ys)
         def _():
-            pass_key(order + 1)
-
-        @pl.when(order + 1 < zs)
+            pass_key(order + AHEAD)
+
+        @pl.when(order + AHEAD < zs)
         def _():
-            pass_value(order + 1)
+            pass_value(order + AHEAD)
 
         y_at = y_of(order)
         key_sibling(y_at, 1 - core).wait_recv()
@@ -281,40 +283,38 @@
             top = jnp.max(scores, axis=0, keepdims=True)
             exp_tile = jnp.exp2((scores - top) * exp_scale)
             exps[y_at, :, lanes] = exp_tile
+            exps_low[y_at, :, lanes] = exp_tile.astype(BF16)
             max_rows[pl.ds(y_at, 1), lanes] = top
             sum_rows[pl.ds(y_at, 1), lanes] = jnp.sum(exp_tile, axis=0, keepdims=True)
         return carry
 
+    for order in range(1, AHEAD):
+        pass_key(jnp.int32(order))
+        pass_value(jnp.int32(order))
     lax.fori_loop(0, ys, score, 0)
-    for order in range(ys + 1, zs):
+    for order in range(ys + AHEAD, zs):
         pass_value(order)
-    for order in range(zs):
-        value_sibling(z_of(order), 1 - core).wait_recv()
-
-    def weigh(y_at, carry):
-        value_wide = value_all[y_at].astype(F32).reshape(keys, HD)
-        value_cols[y_at] = value_wide.T.astype(BF16)
-        value_tile = value_wide.astype(BF16)
-        for first in range(0, cols, step):
-            lanes = slice(first, first + step)
-            weight_grad = matmul(value_tile, grad_cols[:, lanes])
-            grad_weights[y_at, :, lanes] = weight_grad
-            dot_rows[pl.ds(y_at, 1), lanes] = jnp.sum(
-                exps[y_at, :, lanes] * weight_grad, axis=0, keepdims=True
-            )
-        return carry
-
-    lax.fori_loop(0, ys, weigh, 0)
-
     top = jnp.max(max_rows[...], axis=0, keepdims=True)
     factor = jnp.exp2((max_rows[...] - top) * exp_scale)
     ratio_rows[...] = factor
     scale_row[...] = top
-    for index, row in enumerate((
-        top,
-        jnp.sum(sum_rows[...] * factor, axis=0, keepdims=True),
-        jnp.sum(dot_rows[...] * factor, axis=0, keepdims=True),
-    )):
+    total = jnp.sum(sum_rows[...] * factor, axis=0, keepdims=True)
+    for order in range(zs):
+        value_sibling(z_of(order), 1 - core).wait_recv()
+
+    def attend(y_at, carry):
+        value_cols = value_all[y_at].astype(F32).reshape(keys, HD).T.astype(BF16)
+        for first in range(0, cols, step):
+            lanes = slice(first, first + step)
+            attended_acc[:, lanes] += (
+                matmul(value_cols, exps_low[y_at, :, lanes]) * ratio_rows[pl.ds(y_at, 1), lanes]
+            )
+        return carry
+
+    lax.fori_loop(0, ys, attend, 0)
+
+    dots = jnp.sum(attended_acc[...] * grad_cols[...].astype(F32), axis=0, keepdims=True)
+    for index, row in enumerate((top, total, dots)):
         for head_at in range(GROUP):
             stat_all[x, index, head_at:head_at + 1, :] = row[
                 :, head_at * toks:(head_at + 1) * toks
@@ -346,14 +346,14 @@
             query_own(part, lax.rem(x + hop, xs), me).wait_send()
             query_mate(part, lax.rem(x + hop, xs), mate).wait_send()
 
-    def attend(y_at, carry):
+    def weigh(y_at, carry):
+        value_tile = value_all[y_at].astype(F32).reshape(keys, HD).astype(BF16)
         for first in range(0, cols, step):
             lanes = slice(first, first + step)
-            weights = exps[y_at, :, lanes] * ratio_rows[pl.ds(y_at, 1), lanes]
-            attended_acc[:, lanes] += matmul(value_cols[y_at], weights.astype(BF16))
+            grad_weights[y_at, :, lanes] = matmul(value_tile, grad_cols[:, lanes])
         return carry
 
-    lax.fori_loop(0, ys, attend, 0)
+    lax.fori_loop(0, ys, weigh, 0)
 
     for hop in range(1, xs):
         stat_copy(x, lax.rem(x + hop, xs)).wait_recv()
@@ -441,7 +441,7 @@
         value_send[:, order] = (
             kv_part[order, core, 1].astype(F32) + sibling_in[order, 1].astype(F32)
         ).astype(BF16)
-        for near in range(1, zs):
+        for near in reversed(range(1, zs)):
             dvalue_z(order, z_of(near), z).start()
 
     def backward(turn, carry):
@@ -495,7 +495,7 @@
             dvy_ss.at[order], dvy_rs.at[order], at_y(y_of(order)),
         )
 
-    for near in range(1, zs):
+    for near in reversed(range(1, zs)):
         dkey_z(z_of(near), z).start()
     key_home[z] = key_last[z]
     for near in range(1, zs):
@@ -504,11 +504,20 @@
         value_last[:, half] = sum(
             value_in[z_at].astype(F32) for z_at in range(half, zs, 2)
         ).astype(BF16)
-    for order in range(1, ys):
+    for order in reversed(range(1, ys)):
         dvalue_y(order).start()
     value_home[0] = value_last[0]
 
+    for order in range(ys):
+        dsib_copy(order, 1 - core).wait_send()
+        if order:
+            dkey_y(order).wait_send()
+    for order in range(1, zs):
+        dvalue_all(z_of(order), z).wait_send()
     add_out(1, query_out)
+    for part in range(2):
+        for hop in range(1, xs):
+            out_x(part, lax.rem(x + hop, xs), x).wait_send()
     for near in range(1, zs):
         dkey_z(z, z_of(near)).wait_recv()
     for half in range(2):
@@ -526,17 +535,10 @@
         out[:, :, head_lanes(1 - parity, width)] = pair_in[part]
 
     for order in range(1, zs):
-        peer = z_of(order)
-        dkey_z(peer, z).wait_send()
-        dvalue_all(peer, z).wait_send()
-    for order in range(ys):
-        dsib_copy(order, 1 - core).wait_send()
-        if order:
-            dkey_y(order).wait_send()
-            dvalue_y(order).wait_send()
+        dkey_z(z_of(order), z).wait_send()
+    for order in range(1, ys):
+        dvalue_y(order).wait_send()
     for part in range(2):
-        for hop in range(1, xs):
-            out_x(part, lax.rem(x + hop, xs), x).wait_send()
         out_pair(part).wait_send()
 
 
@@ -572,11 +574,11 @@
             vmem((ys,) + value_vectors.shape, BF16),
             vmem((cols, HD), BF16), vmem((cols, HD), BF16),
             vmem((HD, cols), BF16), vmem((HD, cols), BF16),
-            vmem((ys, HD, keys), BF16), vmem((ys, HD, keys), BF16),
+            vmem((ys, HD, keys), BF16),
             vmem((ys, keys, toks), jnp.int32),
-            vmem((ys, keys, cols), F32), vmem((ys, keys, cols), F32),
-            vmem((ys, cols), F32), vmem((ys, cols), F32), vmem((ys, cols), F32),
-            vmem((ys, cols), F32), vmem((1, cols), F32), vmem((1, cols), F32),
+            vmem((ys, keys, cols), F32), vmem((ys, keys, cols), BF16),
+            vmem((ys, keys, cols), F32),
+            vmem((ys, cols), F32), vmem((ys, cols), F32), vmem((ys, cols), F32), vmem((1, cols), F32), vmem((1, cols), F32),
             vmem((xs, 3, GROUP, toks), F32),
             vmem((HD, cols), F32), vmem((HD, cols), F32),
             vmem((2, xs, 2, 2, ROWS, width), BF16), vmem((2, xs, 2, 2, ROWS, width), BF16),

time: 58.8 us -> 58 us (0.986)
  Pallas kernels: 57.7 us -> 56.8 us
    pallas_call x1, Pallas kernels: 56.2 us -> 55.3 us  [shards(): pl.pallas_call(functools.partial(kernel, split), out_shape=results, in_sp...]
where the time goes in v4:
time: 58 us; the launch traced here: 57.4 us
  Pallas kernels  56.8 us (98%)
  between operations  0.64 us (1%)
    pallas_call x1, Pallas kernels, shards(): pl.pallas_call(functools.partial(kernel, split), out_shape=results, in_sp...  55.3 us
    pallas_call x1, Pallas kernels, shards(): pl.pallas_call(finish, out_shape=results, in_specs=[whole] * 4, out_specs...  1.54 us

profile of v4, /device:TPU:1, one launch (start us, length us, event | category | flops | bytes accessed | tf_op | source)
XLA Modules:
  0.0 57.4 jit_solution(10432104409426919627)
XLA Ops:
  0.6 55.3 %attention.1 = (bf16[2,8,2048]{2,1,0:T(8,128)(2,1)}, bf16[2,8,2048]{2,1,0:T(8,128)(2,1)}, bf16[2,8,256]{2,1,0:T(8,128)(2,1)}, bf16[2,8,256]{2,1,0:T(8,128)(2,1)}) custom-call(bf16[2,8,2048]{2,1,0:T(8,128)(2,1)} %query_ref.1, bf16[2,8,2048]{2,1,0:T(8,128)(2,1)} %grad_ref.1, bf16[2,8,256]{2,1,0:T(8,128)(2,1)} %key_ref.1, bf16[2,8,256]{2,1,0:T(8,128)(2,1)} %value_ref.1, ...), custom_call_target="tpu_custom_call" | custom-call | tf_op jit(solution)/shard_map/attention/pallas_call | solution.py:565
  55.9 1.5 %finish.1 = (bf16[2,8,2048]{2,1,0:T(8,128)(2,1)}, bf16[2,8,2048]{2,1,0:T(8,128)(2,1)}, bf16[2,8,256]{2,1,0:T(8,128)(2,1)}, bf16[2,8,256]{2,1,0:T(8,128)(2,1)}) custom-call(bf16[2,8,2048]{2,1,0:T(8,128)(2,1)} %get-tuple-element.8.refs_0_, bf16[2,8,2048]{2,1,0:T(8,128)(2,1)} %get-tuple-element.9.refs_1_, bf16[2,8,256]{2,1,0:T(8,128)(2,1)} %get-tuple-element.10.refs_2_, ...), custom_call_target="tpu_custom_call" | custom-call | tf_op jit(solution)/shard_map/finish/pallas_call | solution.py:604

commit v5 on v4

--- a/solution.py
+++ b/solution.py
@@ -150,7 +150,7 @@
     for part in range(2):
         query_pair(part, me).start()
     for part in range(2):
-        for hop in range(1, xs):
+        for hop in sorted(range(1, xs), key=lambda h: -min(h, xs - h)):
             query_own(part, lax.rem(x + hop, xs), me).start()
     own = [
         pltpu.make_async_copy(
@@ -231,7 +231,7 @@
     own_value.start()
     for part in range(2):
         query_pair(part, mate).wait_recv()
-        for hop in range(1, xs):
+        for hop in sorted(range(1, xs), key=lambda h: -min(h, xs - h)):
             query_mate(part, lax.rem(x + hop, xs), mate).start()
     own_value.wait()
     value_sibling(z, core).start()
@@ -393,7 +393,7 @@
             out_part[part, :, :, :, :, lanes] = (
                 (acc[:, rows] * scale(rows)).T.reshape(xs, 2, 2, ROWS, HD).astype(BF16)
             )
-        for hop in range(1, xs):
+        for hop in sorted(range(1, xs), key=lambda h: -min(h, xs - h)):
             out_x(part, lax.rem(x + hop, xs), x).start()
         out_in[part, x] = out_part[part, x]
 

time: 58 us -> 58 us (level)
  no operation moved by 1% of the time
where the time goes in v5:
time: 58 us; the launch traced here: 57.4 us
  Pallas kernels  56.8 us (98%)
  between operations  0.64 us (1%)
    pallas_call x1, Pallas kernels, shards(): pl.pallas_call(functools.partial(kernel, split), out_shape=results, in_sp...  55.3 us
    pallas_call x1, Pallas kernels, shards(): pl.pallas_call(finish, out_shape=results, in_specs=[whole] * 4, out_specs...  1.54 us

profile of v5, /device:TPU:1, one launch (start us, length us, event | category | flops | bytes accessed | tf_op | source)
XLA Modules:
  0.0 57.4 jit_solution(6529922602780919597)
XLA Ops:
  0.6 55.3 %attention.1 = (bf16[2,8,2048]{2,1,0:T(8,128)(2,1)}, bf16[2,8,2048]{2,1,0:T(8,128)(2,1)}, bf16[2,8,256]{2,1,0:T(8,128)(2,1)}, bf16[2,8,256]{2,1,0:T(8,128)(2,1)}) custom-call(bf16[2,8,2048]{2,1,0:T(8,128)(2,1)} %query_ref.1, bf16[2,8,2048]{2,1,0:T(8,128)(2,1)} %grad_ref.1, bf16[2,8,256]{2,1,0:T(8,128)(2,1)} %key_ref.1, bf16[2,8,256]{2,1,0:T(8,128)(2,1)} %value_ref.1, ...), custom_call_target="tpu_custom_call" | custom-call | tf_op jit(solution)/shard_map/attention/pallas_call | solution.py:565
  55.9 1.5 %finish.1 = (bf16[2,8,2048]{2,1,0:T(8,128)(2,1)}, bf16[2,8,2048]{2,1,0:T(8,128)(2,1)}, bf16[2,8,256]{2,1,0:T(8,128)(2,1)}, bf16[2,8,256]{2,1,0:T(8,128)(2,1)}) custom-call(bf16[2,8,2048]{2,1,0:T(8,128)(2,1)} %get-tuple-element.8.refs_0_, bf16[2,8,2048]{2,1,0:T(8,128)(2,1)} %get-tuple-element.9.refs_1_, bf16[2,8,256]{2,1,0:T(8,128)(2,1)} %get-tuple-element.10.refs_2_, ...), custom_call_target="tpu_custom_call" | custom-call | tf_op jit(solution)/shard_map/finish/pallas_call | solution.py:604
